TPU v7x, 256 devices: a whole 4x4x8 slice. The times are simulated.
256 devices in a mesh: seq: 32 (over y, z), nb: 8 (over x, core).
Axes of the slice: x: 4, y: 4, z: 8, core: 2. Of those that a mesh axis runs over, the one named last changes fastest.
Arguments:
- q_self: bfloat16 [8192, 4096], P('seq', 'nb'), may hold values from -6 to 6
- k_self: bfloat16 [8192, 4096], P('seq', 'nb'), may hold values from -6 to 6
- v_self: bfloat16 [8192, 4096], P('seq', 'nb'), may hold values from -6 to 6
- q_cca: bfloat16 [8192, 4096], P('seq', 'nb'), may hold values from -6 to 6
- memory: bfloat16 [8192, 2, 1024], P('seq'), may hold values from -6 to 6
- database: bfloat16 [65536, 2048], P(('seq', 'nb')), may hold values from -6 to 6
- nbr_block: int32 [2048], P(('seq', 'nb')), may hold values from 0 to 127, as said below
- span_offset: int32 [128], P('seq'), may hold values from 1 to 63
- enc_query: bfloat16 [2048, 1024], P('seq'), may hold values from -0.1355122 to 0.1355122
- enc_out: bfloat16 [1024, 2048], P('seq'), may hold values from -0.1875 to 0.1875
- enc_gain: float32 [2048], replicated, may hold values from 0.5 to 1.5
- cca_kv: bfloat16 [2048, 2, 4096], P(None, None, 'nb'), may hold values from -0.134535646 to 0.134535646
Outputs:
- attended: bfloat16 [8192, 4096], P('seq', 'nb')
Inputs may be any that keep to these rules, and one draw needn't show every extreme that they name: `nbr_block`: block ids are local to a group of 8 devices along nb; the owner of id g is nb index g // 16. Among the 8 requests of one device at most 3 name blocks of one owner, and exactly 3 name blocks of some owner.
All inputs are finite; a program needn't handle non-finite values.
Results may differ from a plain program's by a relative error of at most 0.0041.
Values may be sent and summed in bfloat16 or wider, within the bound.
No kernel may reach another device: no remote copies, remote signals or barrier semaphores. Data moves between devices by JAX's collectives and lax.ppermute only.
A program may use at most 192 MiB of HBM per device.

v0:
```python
import jax
import jax.numpy as jnp
from jax import lax
from jax.experimental import pallas as pl
from jax.experimental.pallas import tpu as pltpu
from jax.sharding import Mesh, PartitionSpec as P


HD = 128
E = 2048
SPAN = 64
ROWS = 256
BLK = 16
DB_DEV = 16
LOG2E = 1.4426950408889634
SCALE = HD ** (-0.5)
MASKED = -1e30
BF = jnp.bfloat16
F32 = jnp.float32

VMEM = pl.BlockSpec(memory_space=pltpu.VMEM)
SMEM = pl.BlockSpec(memory_space=pltpu.SMEM)
ANY = pl.BlockSpec(memory_space=pl.ANY)


def dot(a, b):
    return jnp.dot(a, b, preferred_element_type=F32)


def dot_t(a, b):
    return lax.dot_general(a, b, (((1,), (1,)), ((), ())), preferred_element_type=F32)


def params(mib):
    return pltpu.CompilerParams(vmem_limit_bytes=mib << 20)


def pack_kernel(where, q, k, v, keep, send):
    c = where[2]
    for out, half in ((keep, c), (send, 1 - c)):
        rows = pl.ds(pl.multiple_of(half * 128, 128), 128)
        for j in range(4):
            cols = slice(j * 128, j * 128 + 128)
            out[j, 0] = q[rows, cols]
            out[j, 1] = k[rows, cols]
            out[j, 2] = v[rows, cols].T


def pack(where, q, k, v):
    o = jax.ShapeDtypeStruct((4, 3, 128, 128), BF)
    return pl.pallas_call(
        pack_kernel,
        out_shape=(o, o),
        in_specs=[SMEM] + [VMEM] * 3,
        out_specs=(VMEM, VMEM),
        name="pack",
    )(where, q, k, v)


def flash_step(keys, values, q, state, mask=None):
    s = dot_t(keys, q)
    if mask is not None:
        s = jnp.where(mask, s, MASKED)
    top = jnp.max(s, axis=0, keepdims=True)
    if state is None:
        new_max = top
    else:
        old_max, old_sum, acc = state
        new_max = jnp.maximum(old_max, top)
    p = jnp.exp2((s - new_max) * (SCALE * LOG2E))
    total = jnp.sum(p, axis=0, keepdims=True)
    out = dot(values, p.astype(BF))
    if state is None:
        return new_max, total, out
    shrink = jnp.exp2((old_max - new_max) * (SCALE * LOG2E))
    return new_max, old_sum * shrink + total, acc * shrink + out


def tiles(refs, places):
    keys = jnp.concatenate([ref[t, 0] for t in places for ref in refs], axis=0)
    values = jnp.concatenate([ref[t, 1] for t in places for ref in refs], axis=1)
    return keys, values


def near_kernel(where, q, kv, sib, acc_o, m_o, l_o):
    c = where[2]
    row = lax.broadcasted_iota(jnp.int32, (256, 128), 0)
    col = lax.broadcasted_iota(jnp.int32, (256, 128), 1)
    mask = jnp.where(row < 128, (row <= col).astype(jnp.int32), c) > 0
    for z in range(8):
        state = flash_step(*tiles((kv, sib), (z,)), q[z], None, mask)
        for lo in range(0, z, 2):
            state = flash_step(*tiles((kv, sib), range(lo, min(lo + 2, z))), q[z], state)
        m_o[z] = jnp.broadcast_to(state[0], (8, 128))
        l_o[z] = jnp.broadcast_to(state[1], (8, 128))
        acc_o[z] = state[2]


def near(where, q, kv, sib):
    f = jax.ShapeDtypeStruct((8, 128, 128), F32)
    g = jax.ShapeDtypeStruct((8, 8, 128), F32)
    return pl.pallas_call(
        near_kernel,
        out_shape=(f, g, g),
        in_specs=[SMEM] + [VMEM] * 3,
        out_specs=(VMEM, VMEM, VMEM),
        compiler_params=params(40),
        name="near",
    )(where, q, kv, sib)


def far_kernel(where, q, kv1, sib1, kv2, sib2, kv3, sib3, acc_i, m_i, l_i, out, acc_s, m_s, l_s):
    y = where[0]
    acc_s[...] = acc_i[...]
    m_s[...] = m_i[...]
    l_s[...] = l_i[...]
    for r, refs in enumerate(((kv1, sib1), (kv2, sib2), (kv3, sib3))):

        def row(i, carry, refs=refs):
            zs = (2 * i, 2 * i + 1)
            states = [(m_s[z][:1], l_s[z][:1], acc_s[z]) for z in zs]
            for lo in (0, 4):
                keys, values = tiles(refs, range(lo, lo + 4))
                states = [flash_step(keys, values, q[z], st) for z, st in zip(zs, states)]
            for z, state in zip(zs, states):
                m_s[z] = jnp.broadcast_to(state[0], (8, 128))
                l_s[z] = jnp.broadcast_to(state[1], (8, 128))
                acc_s[z] = state[2]
            return carry

        @pl.when(y > r)
        def _(row=row):
            lax.fori_loop(0, 4, row, 0)

    for z in range(8):
        out[z] = (acc_s[z] / l_s[z][:1]).T.astype(BF)


def far(where, q, pairs, acc, m, l):
    return pl.pallas_call(
        far_kernel,
        out_shape=jax.ShapeDtypeStruct((8, 128, 128), BF),
        in_specs=[SMEM] + [VMEM] * 10,
        out_specs=VMEM,
        scratch_shapes=[
            pltpu.VMEM((8, 128, 128), F32),
            pltpu.VMEM((8, 8, 128), F32),
            pltpu.VMEM((8, 8, 128), F32),
        ],
        compiler_params=params(40),
        name="far",
    )(where, q, *pairs, acc, m, l)


def prep_kernel(enc_out, weight, encq, out):
    w2 = dot(enc_out[...], weight[...]).astype(BF)
    eq = jnp.concatenate([encq[j * 8 : j * 8 + 8] for j in range(8)], axis=1)
    for z in range(8):
        out[z, :32] = w2
        out[z, 32:] = eq


def prep(enc_out, weight, encq):
    return pl.pallas_call(
        prep_kernel,
        out_shape=jax.ShapeDtypeStruct((8, 40, 1024), BF),
        in_specs=[VMEM] * 3,
        out_specs=VMEM,
        compiler_params=params(24),
        name="prep",
    )(enc_out, weight, encq)


def gather_kernel(src, blk, *refs):
    blocks, x = refs[:8], refs[8]

    def fetch(i, carry):
        def copy(ref):
            at = pl.ds(pl.multiple_of(blk[i] * BLK, BLK), BLK)
            x[pl.ds(pl.multiple_of(i * BLK, BLK), BLK)] = ref[at]

        for side in range(2):

            @pl.when((src[i] >= 4) == (side == 1))
            def _(side=side):
                for a in range(4):

                    @pl.when(src[i] == side * 4 + a)
                    def _(a=a):
                        copy(blocks[side * 4 + a])

        return carry

    lax.fori_loop(0, 64, fetch, 0)


def gather(src, blk, blocks):
    return pl.pallas_call(
        gather_kernel,
        out_shape=jax.ShapeDtypeStruct((1024, E), BF),
        in_specs=[SMEM] * 2 + [VMEM] * 8,
        out_specs=VMEM,
        compiler_params=params(24),
        name="gather",
    )(src, blk, *blocks)


def encode_kernel(off, where, x, e0, e1, e2, e3, gain, mem_k, mem_v, ctx, encq):
    y = where[0]
    for r, ref in enumerate((e0, e1, e2, e3)):
        for z in range(8):
            for j in range(8):
                piece = ref[z, 32:, j * 128 : j * 128 + 128]
                encq[lax.rem(y + 4 - r, 4), z * 64 + j * 8 : z * 64 + j * 8 + 8] = piece

    def encode_span(span, carry):
        rows = pl.ds(pl.multiple_of(span * ROWS, ROWS), ROWS)
        wide = x[rows].astype(F32)
        mean = jnp.mean(wide * wide, axis=1, keepdims=True)
        h = (wide * lax.rsqrt(mean + 1e-6) * gain[...]).astype(BF)
        eq = (dot(h, encq[...].reshape(E, HD)) * SCALE).astype(BF)
        tokens = pl.ds(pl.multiple_of(span * SPAN, SPAN), SPAN)
        s = dot_t(eq, mem_k[tokens])
        seen = lax.broadcasted_iota(jnp.int32, (ROWS, SPAN), 1) < off[span]
        s = jnp.where(seen, s, MASKED)
        top = jnp.max(s, axis=1, keepdims=True)
        p = jnp.where(seen, jnp.exp(s - top), 0.0)
        total = jnp.sum(p, axis=1, keepdims=True)
        ctx[rows] = (dot(p.astype(BF), mem_v[tokens]) / total).astype(BF)
        return carry

    lax.fori_loop(0, 4, encode_span, 0)


def encode(off, where, x, encq, gain, mem_k, mem_v):
    return pl.pallas_call(
        encode_kernel,
        out_shape=jax.ShapeDtypeStruct((1024, 128), BF),
        in_specs=[SMEM] * 2 + [VMEM] * 8,
        out_specs=VMEM,
        scratch_shapes=[pltpu.VMEM((4, 512, 128), BF)],
        compiler_params=params(24),
        name="encode",
    )(off, where, x, *encq, gain, mem_k, mem_v)


def attend(q, keys, values):
    s = dot_t(q, keys) * (SCALE * LOG2E)
    p = jnp.exp2(s - jnp.max(s, axis=1, keepdims=True))
    return dot(p.astype(BF), values) / jnp.sum(p, axis=1, keepdims=True)


def cross_body(spans, where, kvx, ctx, w2s, q, qn, own_o, ear_o, w2):
    y, x, c = where[0], where[1], where[2]
    for turned in range(4):
        r = lax.rem(x - y + turned + 4, 4)
        for side, cc in ((0, c), (1, 1 - c)):
            for z in range(4):
                w2[side, r, z * 32 : z * 32 + 32] = w2s[turned][4 * cc + z, :32]

    def cross_span(at, carry):
        span = spans[0] + at
        rows = pl.ds(pl.multiple_of(span * ROWS, ROWS), ROWS)
        context = jnp.concatenate([ref[rows] for ref in ctx], axis=1)
        kv = kvx[pl.ds(pl.multiple_of(at * ROWS, ROWS), ROWS)]
        kv = (kv + dot(context, w2[...].reshape(1024, 1024))).astype(BF)
        mine = q[pl.ds(pl.multiple_of(span * SPAN, SPAN), SPAN)]
        if spans[0] == 3:
            later = qn[...]
        else:
            later = q[pl.ds(pl.multiple_of((span + 1) * SPAN, SPAN), SPAN)]
        both = jnp.concatenate([mine, later], axis=0)
        at_rows = pl.ds(pl.multiple_of(at * SPAN, SPAN), SPAN)
        for j in range(4):
            cols = slice(j * 128, j * 128 + 128)
            out = attend(both[:, cols], kv[:, cols], kv[:, 512 + j * 128 : 640 + j * 128])
            own_o[at_rows, cols] = out[:SPAN]
            ear_o[at_rows, cols] = out[SPAN:]
        return carry

    lax.fori_loop(0, len(spans), cross_span, 0)


def cross(spans, where, kvx, ctx, w2s, q, qn):
    def body(where, kvx, *refs):
        cross_body(spans, where, kvx, refs[:8], refs[8:12], *refs[12:])

    o = jax.ShapeDtypeStruct((len(spans) * SPAN, 512), F32)
    kv_block = pl.BlockSpec(
        (len(spans) * ROWS, 1024), (lambda i: (3, 0)) if spans[0] == 3 else (lambda i: (0, 0))
    )

    def whole(a):
        return pl.BlockSpec(a.shape, lambda i: (0,) * a.ndim)

    return pl.pallas_call(
        body,
        out_shape=(o, o),
        grid=(1,),
        in_specs=[SMEM, kv_block] + [whole(a) for a in (*ctx, *w2s, q, qn)],
        out_specs=(whole(o), whole(o)),
        scratch_shapes=[pltpu.VMEM((2, 4, 128, 1024), BF)],
        compiler_params=params(40),
        name="cross",
    )(where, kvx, *ctx, *w2s, q, qn)


def final_kernel(off, attn, own_a, own_b, ear_a, recv, out):
    pos = lax.broadcasted_iota(jnp.int32, (SPAN, 512), 0)
    for span in range(4):
        own = own_b[...] if span == 3 else own_a[span * SPAN : span * SPAN + SPAN]
        ear = recv[...] if span == 0 else ear_a[(span - 1) * SPAN : span * SPAN]
        cca = jnp.where(pos >= off[span], own, ear)
        rows = slice((span % 2) * SPAN, (span % 2) * SPAN + SPAN)
        self_out = jnp.concatenate([attn[span // 2, j, rows] for j in range(4)], axis=1)
        out[span * SPAN : span * SPAN + SPAN] = (self_out.astype(F32) + cca).astype(BF)


def final(off, attn, own_a, own_b, ear_a, recv):
    return pl.pallas_call(
        final_kernel,
        out_shape=jax.ShapeDtypeStruct((256, 512), BF),
        in_specs=[SMEM] + [VMEM] * 5,
        out_specs=VMEM,
        name="final",
    )(off, attn, own_a, own_b, ear_a, recv)


def swap(a, axis):
    return lax.all_to_all(a, axis, split_axis=0, concat_axis=0, tiled=True)


def sibling(a):
    return lax.ppermute(a, "c", [(0, 1), (1, 0)])


def turn(a, axis, distance):
    n = lax.axis_size(axis)
    return lax.ppermute(a, axis, [(i, (i + distance) % n) for i in range(n)])


def onward(a, axis, distance):
    n = lax.axis_size(axis)
    return lax.ppermute(a, axis, [(i, i + distance) for i in range(n - distance)])


def block(
    q_self, k_self, v_self, q_cca, memory, database, nbr_block, span_offset,
    enc_query, enc_out, enc_gain, cca_kv,
):
    y, x, c = lax.axis_index("y"), lax.axis_index("x"), lax.axis_index("c")
    where = jnp.stack([y, x, c]).astype(jnp.int32)
    nb = 2 * x + c
    steps = lax.axis_size("y") * lax.axis_size("z")

    pair = jnp.stack([nbr_block, sibling(nbr_block)])
    keep, send = pack(where, q_self, k_self, v_self)
    send = sibling(send)
    first, second = jnp.where(c == 0, keep, send), jnp.where(c == 0, send, keep)
    qkv = jnp.concatenate([first, second])
    pairs = jnp.stack([pair] + [turn(pair, "x", r) for r in (1, 2, 3)])
    blocks = [database] + [turn(database, "x", r) for r in (1, 2, 3)]
    blocks = blocks + [sibling(database)]
    blocks = blocks + [sibling(b) for b in blocks[1:4]]
    qn = lax.ppermute(q_cca[:SPAN], ("y", "z"), [(i, i - 1) for i in range(1, steps)])

    qkv = swap(qkv, "z")
    weight = cca_kv.reshape(E, 1024)
    encq = lax.dynamic_slice(enc_query, (0, nb * HD), (64, HD))
    bundle = prep(enc_out, weight, encq)
    qkv, bundle = lax.optimization_barrier((qkv, bundle))
    q, kv = qkv[:, 0], qkv[:, 1:]
    kvs = [kv] + [onward(kv, "y", r) for r in (1, 2, 3)]
    sibs = [sibling(kv)]
    sibs = sibs + [sibling(a) for a in kvs[1:]]

    bundle = swap(bundle, "z")
    bundles = [bundle] + [turn(bundle, "y", r) for r in (1, 2, 3)]

    near_out = near(where, q, kv, sibs[0])
    pairs, qn, _ = lax.optimization_barrier((pairs, qn, near_out[1]))
    ours = jnp.arange(4, dtype=jnp.int32)
    ids = pairs[(x - ours) % 4]
    ids = jnp.where(c == 0, ids, ids[:, ::-1]).reshape(-1)
    owner = ids // DB_DEV
    slot = ids % DB_DEV
    src = (x - owner // 2) % 4 + 4 * (owner % 2 != c)
    rows = gather(src.astype(jnp.int32), slot.astype(jnp.int32), blocks)
    kvx = dot(rows, weight)

    mem = lax.dynamic_slice(memory, (0, 0, nb * HD), (256, 2, HD))
    ctx = encode(span_offset, where, rows, bundles, enc_gain.reshape(1, E), mem[:, 0], mem[:, 1])
    ctxs = [ctx] + [turn(ctx, "x", r) for r in (1, 2, 3)]
    ctxs = ctxs + [sibling(ctx)]
    ctxs = ctxs + [sibling(a) for a in ctxs[1:4]]
    halves = [a for r in (1, 2, 3) for a in (kvs[r], sibs[r])]
    attn = far(where, q, halves, *near_out)
    back = swap(attn, "z").reshape(2, 4, 128, 128)
    own_b, rem = cross((3,), where, kvx, ctxs, bundles, q_cca, qn)
    recv = lax.ppermute(rem, ("y", "z"), [(i, i + 1) for i in range(steps - 1)])
    back = swap(back, "c")
    own_a, ear_a = cross((0, 1, 2), where, kvx, ctxs, bundles, q_cca, qn)
    return final(span_offset, back, own_a, own_b, ear_a, recv)


def solution(mesh):
    fine = Mesh(mesh.devices.reshape(4, 8, 4, 2), ("y", "z", "x", "c"))
    s, n = ("y", "z"), ("x", "c")
    in_specs = (
        P(s, n), P(s, n), P(s, n), P(s, n),
        P(s, None, None),
        P((*s, *n), None),
        P((*s, *n)),
        P(s),
        P(s, None),
        P(s, None),
        P(),
        P(None, None, n),
    )
    return jax.shard_map(block, mesh=fine, in_specs=in_specs, out_specs=P(s, n), check_vma=False)
```

profile of v0, /device:TPU:25, one launch (start us, length us, event | category | flops | bytes accessed | tf_op | source)
XLA Modules:
  0.0 218.2 jit_solution(13221526340392244897)
XLA Ops:
  0.6 2.1 pack.1
  3.4 1.6 collective-permute-done
  7.0 8.2 %all-to-all-start = ((bf16[8,3,128,128]{3,2,1,0:T(8,128)(2,1)}), bf16[8,3,128,128]{3,2,1,0:T(8,128)(2,1)}, u32[]{:S(2)}, u32[]{:S(2)}) async-start(bf16[8,3,128,128]{3,2,1,0:T(8,128)(2,1)} %pad_maximum_fusion), calls=%async_computation | async-start | bytes 1572864 | tf_op jit(solution)/shard_map/all_to_all | solution.py:330
  15.2 1.3 collective-permute-start.13
  16.5 2.5 %collective-permute-start.14 = (bf16[256,2048]{1,0:T(8,128)(2,1)S(1)}, bf16[256,2048]{1,0:T(8,128)(2,1)}, u32[]{:S(2)}, u32[]{:S(2)}) collective-permute-start(bf16[256,2048]{1,0:T(8,128)(2,1)S(1)} %copy-done.6), channel_id=1, source_target_pairs={{0,4},{2,6},{4,0},{6,2},{1,5},{3,7},{5,1},{7,3},{8,12},{10,14},{12... | collective-permute-start | bytes 3145736 | tf_op jit(solution)/shard_map/ppermute | solution.py:339
  18.9 1.2 collective-permute-start.15
  20.1 1.5 collective-permute-start.16
  21.6 19.0 %collective-permute-done.13.refs_1_ = bf16[256,2048]{1,0:T(8,128)(2,1)S(1)} collective-permute-done((bf16[256,2048]{1,0:T(8,128)(2,1)S(1)}, bf16[256,2048]{1,0:T(8,128)(2,1)S(1)}, u32[]{:S(2)}, u32[]{:S(2)}) %collective-permute-start.13) | collective-permute-done | bytes 1048608 | tf_op jit(solution)/shard_map/ppermute | solution.py:339
  40.5 1.6 collective-permute-start.17
  42.2 3.4 %copy.17 = bf16[256,8,2,512]{3,1,2,0:T(8,128)(2,1)S(1)} copy(bf16[256,8,2,512]{3,2,1,0:T(2,128)(2,1)} %bitcast.30) | data formatting | bytes 8388608
  45.6 1.7 prep.1
  47.4 2.0 copy-done.4
  49.4 6.8 %all-to-all-start.3 = ((bf16[8,40,1024]{2,1,0:T(8,128)(2,1)}), bf16[8,40,1024]{2,1,0:T(8,128)(2,1)S(1)}, u32[]{:S(2)}, u32[]{:S(2)}) async-start(bf16[8,40,1024]{2,1,0:T(8,128)(2,1)} %prep.1), calls=%async_computation.3 | async-start | bytes 1310720 | tf_op jit(solution)/shard_map/all_to_all | solution.py:330
  56.2 7.9 %collective-permute-done.14.refs_2_ = bf16[256,2048]{1,0:T(8,128)(2,1)} collective-permute-done((bf16[256,2048]{1,0:T(8,128)(2,1)S(1)}, bf16[256,2048]{1,0:T(8,128)(2,1)}, u32[]{:S(2)}, u32[]{:S(2)}) %collective-permute-start.14) | collective-permute-done | bytes 1048608 | tf_op jit(solution)/shard_map/ppermute | solution.py:339
  64.1 1.5 collective-permute-start.18
  66.1 3.6 %collective-permute-done.8 = s32[8]{0:T(128)S(1)} collective-permute-done((s32[8]{0:T(128)S(1)}, s32[8]{0:T(128)S(1)}, u32[]{:S(2)}, u32[]{:S(2)}) %collective-permute-start.8) | collective-permute-done | bytes 64 | tf_op jit(solution)/shard_map/ppermute | solution.py:334
  70.2 1.9 collective-permute-done.11
  72.1 1.2 collective-permute-start.10
  73.3 3.0 %collective-permute-done.10 = s32[2,8]{1,0:T(2,128)S(1)} collective-permute-done((s32[2,8]{1,0:T(2,128)S(1)}, s32[2,8]{1,0:T(2,128)S(1)}, u32[]{:S(2)}, u32[]{:S(2)}) %collective-permute-start.10) | collective-permute-done | bytes 96 | tf_op jit(solution)/shard_map/ppermute | solution.py:339
  76.4 3.6 %collective-permute-done.9 = s32[2,8]{1,0:T(2,128)S(1)} collective-permute-done((s32[2,8]{1,0:T(2,128)S(1)}, s32[2,8]{1,0:T(2,128)S(1)}, u32[]{:S(2)}, u32[]{:S(2)}) %collective-permute-start.9) | collective-permute-done | bytes 96 | tf_op jit(solution)/shard_map/ppermute | solution.py:339
  80.0 4.7 %collective-permute-start.12 = (bf16[64,512]{1,0:T(8,128)(2,1)S(1)}, bf16[64,512]{1,0:T(8,128)(2,1)S(1)}, u32[]{:S(2)}, u32[]{:S(2)}) collective-permute-start(bf16[64,512]{1,0:T(8,128)(2,1)S(1)} %slice.17), channel_id=1, source_target_pairs={{8,0},{16,8},{24,16},{32,24},{40,32},{48,40},{56,48},{64,56},{72,6... | collective-permute-start | bytes 196616 | tf_op jit(solution)/shard_map/ppermute | solution.py:365
  84.7 1.3 constant_dynamic-slice_fusion.1
  86.0 1.9 slice.16.kv
  88.5 1.3 collective-permute-start.1
  89.8 1.3 collective-permute-start.3
  91.1 4.0 %collective-permute-start.7 = (bf16[8,2,128,128]{3,2,1,0:T(8,128)(2,1)}, bf16[8,2,128,128]{3,2,1,0:T(8,128)(2,1)S(1)}, u32[]{:S(2)}, u32[]{:S(2)}) collective-permute-start(bf16[8,2,128,128]{3,2,1,0:T(8,128)(2,1)} %slice.16.kv), channel_id=1, source_target_pairs={{0,1},{1,0},{2,3},{3,2},{4,5},{5,4},{6,7},{7,6},{8,9},{9,8},{10,11... | collective-permute-start | bytes 1572872 | tf_op jit(solution)/shard_map/ppermute | solution.py:334
  95.1 6.4 %collective-permute-start.20 = (bf16[8,40,1024]{2,1,0:T(8,128)(2,1)S(1)}, bf16[8,40,1024]{2,1,0:T(8,128)(2,1)S(1)}, u32[]{:S(2)}, u32[]{:S(2)}) collective-permute-start(bf16[8,40,1024]{2,1,0:T(8,128)(2,1)S(1)} %all-to-all-done.3.e0.refs_8_), channel_id=1, source_target_pairs={{0,64},{64,128},{128,192},{192,0},{1,65},{65,129},{129,193},{193,1... | collective-permute-start | bytes 1966088 | tf_op jit(solution)/shard_map/ppermute | solution.py:339
  101.6 1.5 collective-permute-start.5
  103.7 5.7 %collective-permute-start.2 = (bf16[8,2,128,128]{3,2,1,0:T(8,128)(2,1)}, bf16[8,2,128,128]{3,2,1,0:T(8,128)(2,1)}, u32[]{:S(2)}, u32[]{:S(2)}) collective-permute-start(bf16[8,2,128,128]{3,2,1,0:T(8,128)(2,1)} %collective-permute-done.1.kv1), channel_id=1, source_target_pairs={{0,1},{1,0},{2,3},{3,2},{4,5},{5,4},{6,7},{7,6},{8,9},{9,8},{10,11... | collective-permute-start | bytes 1572872 | tf_op jit(solution)/shard_map/ppermute | solution.py:334
  109.4 10.4 %collective-permute-start.21 = (bf16[8,40,1024]{2,1,0:T(8,128)(2,1)S(1)}, bf16[8,40,1024]{2,1,0:T(8,128)(2,1)S(1)}, u32[]{:S(2)}, u32[]{:S(2)}) collective-permute-start(bf16[8,40,1024]{2,1,0:T(8,128)(2,1)S(1)} %all-to-all-done.3.e0.refs_8_), channel_id=1, source_target_pairs={{0,128},{64,192},{128,0},{192,64},{1,129},{65,193},{129,1},{193,65... | collective-permute-start | bytes 1966088 | tf_op jit(solution)/shard_map/ppermute | solution.py:339
  123.5 3.1 %near.1 = (f32[8,128,128]{2,1,0:T(8,128)S(1)}, f32[8,8,128]{2,1,0:T(8,128)S(1)}, f32[8,8,128]{2,1,0:T(8,128)S(1)}) custom-call(s32[3]{0:T(128)S(1)} %copy-done.34, bf16[8,128,128]{2,1,0:T(8,128)(2,1)S(1)} %slice_bitcast_fusion.q, bf16[8,2,128,128]{3,2,1,0:T(8,128)(2,1)} %slice.16.kv, bf16[8,2,128,128]{3,2,1,0:T(8,128)(2,1)S(1)} %copy-done.20), custom_call_target="tpu_custom_call" | custom-call | tf_op jit(solution)/shard_map/near/pallas_call | solution.py:102
  128.8 1.2 copy-done.7
  130.0 1.2 copy-done.9
  131.2 6.5 %gather.7.x = bf16[1024,2048]{1,0:T(8,128)(2,1)S(1)} custom-call(s32[64]{0:T(128)S(1)} %get-tuple-element.38.src, s32[64]{0:T(128)S(1)} %get-tuple-element.37.blk, bf16[256,2048]{1,0:T(8,128)(2,1)S(1)} %copy-done.7, bf16[256,2048]{1,0:T(8,128)(2,1)S(1)} %copy-done.9, bf16[256,2048]{1,0:T(8,128)(2,1)} %collective-permute-done.14.refs_2_, ...), custom_call_target="tpu_custom_call" | custom-call | tf_op jit(solution)/shard_map/gather/pallas_call | solution.py:198
  137.8 11.2 %collective-permute-done.22.e3.refs_11_ = bf16[8,40,1024]{2,1,0:T(8,128)(2,1)S(1)} collective-permute-done((bf16[8,40,1024]{2,1,0:T(8,128)(2,1)S(1)}, bf16[8,40,1024]{2,1,0:T(8,128)(2,1)S(1)}, u32[]{:S(2)}, u32[]{:S(2)}) %collective-permute-start.22) | collective-permute-done | bytes 655392 | tf_op jit(solution)/shard_map/ppermute | solution.py:339
  149.1 4.7 %encode.1.refs_0_ = bf16[1024,128]{1,0:T(8,128)(2,1)S(1)} custom-call(s32[4]{0:T(128)S(1)} %copy-done.36, s32[3]{0:T(128)S(1)} %copy-done.34, bf16[1024,2048]{1,0:T(8,128)(2,1)S(1)} %gather.7.x, bf16[8,40,1024]{2,1,0:T(8,128)(2,1)S(1)} %all-to-all-done.3.e0.refs_8_, bf16[8,40,1024]{2,1,0:T(8,128)(2,1)S(1)} %collective-permute-done.20.e1.refs_9_, ...), custom_call_target="tpu_custom_call" | custom-call | tf_op jit(solution)/shard_map/encode/pallas_call | solution.py:236
  153.8 2.0 copy-done.1
  155.8 1.7 collective-permute-start.24
  158.5 18.6 %far.1 = bf16[8,128,128]{2,1,0:T(8,128)(2,1)S(1)} custom-call(s32[3]{0:T(128)S(1)} %copy-done.34, bf16[8,128,128]{2,1,0:T(8,128)(2,1)S(1)} %slice_bitcast_fusion.q, bf16[8,2,128,128]{3,2,1,0:T(8,128)(2,1)} %collective-permute-done.1.kv1, bf16[8,2,128,128]{3,2,1,0:T(8,128)(2,1)} %collective-permute-done.2.sib1, ...), custom_call_target="tpu_custom_call" | custom-call | tf_op jit(solution)/shard_map/far/pallas_call | solution.py:140
  177.8 4.2 %all-to-all-start.1 = ((bf16[8,128,128]{2,1,0:T(8,128)(2,1)}), bf16[8,128,128]{2,1,0:T(8,128)(2,1)}, u32[]{:S(2)}, u32[]{:S(2)}) async-start(bf16[8,128,128]{2,1,0:T(8,128)(2,1)} %copy-done.16), calls=%async_computation.1 | async-start | bytes 524288 | tf_op jit(solution)/shard_map/all_to_all | solution.py:330
  182.0 1.6 collective-permute-start.26
  184.2 7.5 %fusion.5.kvx = f32[1024,1024]{1,0:T(8,128)S(1)} fusion(bf16[1024,2048]{1,0:T(8,128)(2,1)} %copy-done.1, bf16[2048,1024]{1,0:T(8,128)(2,1)} %bitcast.28), kind=kOutput, calls=%fused_computation.38 | convolution fusion | flops 4294967296 | bytes 12582912 | tf_op jit(solution)/shard_map/dot_general | solution.py:27
  191.8 3.7 %cross.3 = (f32[64,512]{1,0:T(8,128)S(1)}, f32[64,512]{1,0:T(8,128)}) custom-call(s32[3]{0:T(128)S(1)} %copy-done.34, f32[1024,1024]{1,0:T(8,128)S(1)} %fusion.5.kvx, bf16[1024,128]{1,0:T(8,128)(2,1)S(1)} %encode.1.refs_0_, bf16[1024,128]{1,0:T(8,128)(2,1)} %collective-permute-done.23.refs_1_, bf16[1024,128]{1,0:T(8,128)(2,1)} %collective-permute-done.24.refs_2_, ...), custom_call_target="tpu_custom_call" | custom-call | tf_op jit(solution)/shard_map/cross/pallas_call | solution.py:296
  196.2 3.3 %collective-permute-start.30 = (f32[64,512]{1,0:T(8,128)}, f32[64,512]{1,0:T(8,128)}, u32[]{:S(2)}, u32[]{:S(2)}) collective-permute-start(f32[64,512]{1,0:T(8,128)} %get-tuple-element.30), channel_id=1, source_target_pairs={{0,8},{8,16},{16,24},{24,32},{32,40},{40,48},{48,56},{56,64},{64,7... | collective-permute-start | bytes 393224 | tf_op jit(solution)/shard_map/ppermute | solution.py:400
  199.5 4.8 %all-to-all-start.2 = ((bf16[2,4,128,128]{3,2,1,0:T(8,128)(2,1)}), bf16[2,4,128,128]{3,2,1,0:T(8,128)(2,1)}, u32[]{:S(2)}, u32[]{:S(2)}) async-start(bf16[2,4,128,128]{3,2,1,0:T(8,128)(2,1)} %bitcast.4), calls=%async_computation.2 | async-start | bytes 524288 | tf_op jit(solution)/shard_map/all_to_all | solution.py:330
  204.3 2.2 %copy-done.3 = f32[1024,1024]{1,0:T(8,128)S(1)} copy-done((f32[1024,1024]{1,0:T(8,128)S(1)}, f32[1024,1024]{1,0:T(8,128)}, u32[]{:S(2)}) %copy-start.3) | copy-done | bytes 4194328
  210.2 4.5 %cross.2 = (f32[192,512]{1,0:T(8,128)S(1)}, f32[192,512]{1,0:T(8,128)S(1)}) custom-call(s32[3]{0:T(128)S(1)} %copy-done.34, f32[1024,1024]{1,0:T(8,128)S(1)} %copy-done.3, bf16[1024,128]{1,0:T(8,128)(2,1)S(1)} %encode.1.refs_0_, bf16[1024,128]{1,0:T(8,128)(2,1)} %collective-permute-done.23.refs_1_, bf16[1024,128]{1,0:T(8,128)(2,1)} %collective-permute-done.24.refs_2_, ...), custom_call_target="tpu_custom_call" | custom-call | tf_op jit(solution)/shard_map/cross/pallas_call | solution.py:296
  216.2 2.0 final.1
  (127 shorter events, 19.7 us)
Async XLA Ops:
  0.0 42.2 %copy-start = (bf16[64,1024]{1,0:T(8,128)(2,1)S(1)}, bf16[64,1024]{1,0:T(8,128)(2,1)}, u32[]{:S(2)}) copy-start(bf16[64,1024]{1,0:T(8,128)(2,1)} %param.20) | copy-start | bytes 393220
  0.0 15.2 %copy-start.6 = (bf16[256,2048]{1,0:T(8,128)(2,1)S(1)}, bf16[256,2048]{1,0:T(8,128)(2,1)}, u32[]{:S(2)}) copy-start(bf16[256,2048]{1,0:T(8,128)(2,1)} %refs_0_.1) | copy-start | bytes 3145732
  2.7 2.2 %collective-permute-start = (bf16[4,3,128,128]{3,2,1,0:T(8,128)(2,1)}, bf16[4,3,128,128]{3,2,1,0:T(8,128)(2,1)S(1)}, u32[]{:S(2)}, u32[]{:S(2)}) collective-permute-start(bf16[4,3,128,128]{3,2,1,0:T(8,128)(2,1)} %get-tuple-element.19), channel_id=1, source_target_pairs={{0,1},{1,0},{2,3},{3,2},{4,5},{5,4},{6,7},{7,6},{8,9},{9,8},{10,11... | collective-permute-start | bytes 1179656 | tf_op jit(solution)/shard_map/ppermute | solution.py:334
  7.0 42.4 %all-to-all-start = ((bf16[8,3,128,128]{3,2,1,0:T(8,128)(2,1)}), bf16[8,3,128,128]{3,2,1,0:T(8,128)(2,1)}, u32[]{:S(2)}, u32[]{:S(2)}) async-start(bf16[8,3,128,128]{3,2,1,0:T(8,128)(2,1)} %pad_maximum_fusion), calls=%async_computation | async-start | bytes 1572864 | tf_op jit(solution)/shard_map/all_to_all | solution.py:330
  15.2 25.3 %collective-permute-start.13 = (bf16[256,2048]{1,0:T(8,128)(2,1)S(1)}, bf16[256,2048]{1,0:T(8,128)(2,1)S(1)}, u32[]{:S(2)}, u32[]{:S(2)}) collective-permute-start(bf16[256,2048]{1,0:T(8,128)(2,1)S(1)} %copy-done.6), channel_id=1, source_target_pairs={{0,2},{2,4},{4,6},{6,0},{1,3},{3,5},{5,7},{7,1},{8,10},{10,12},{12... | collective-permute-start | bytes 3145736 | tf_op jit(solution)/shard_map/ppermute | solution.py:339
  16.5 47.6 %collective-permute-start.14 = (bf16[256,2048]{1,0:T(8,128)(2,1)S(1)}, bf16[256,2048]{1,0:T(8,128)(2,1)}, u32[]{:S(2)}, u32[]{:S(2)}) collective-permute-start(bf16[256,2048]{1,0:T(8,128)(2,1)S(1)} %copy-done.6), channel_id=1, source_target_pairs={{0,4},{2,6},{4,0},{6,2},{1,5},{3,7},{5,1},{7,3},{8,12},{10,14},{12... | collective-permute-start | bytes 3145736 | tf_op jit(solution)/shard_map/ppermute | solution.py:339
  18.9 46.7 %collective-permute-start.15 = (bf16[256,2048]{1,0:T(8,128)(2,1)S(1)}, bf16[256,2048]{1,0:T(8,128)(2,1)}, u32[]{:S(2)}, u32[]{:S(2)}) collective-permute-start(bf16[256,2048]{1,0:T(8,128)(2,1)S(1)} %copy-done.6), channel_id=1, source_target_pairs={{0,6},{2,0},{4,2},{6,4},{1,7},{3,1},{5,3},{7,5},{8,14},{10,8},{12,... | collective-permute-start | bytes 3145736 | tf_op jit(solution)/shard_map/ppermute | solution.py:339
  20.1 69.8 %collective-permute-start.16 = (bf16[256,2048]{1,0:T(8,128)(2,1)S(1)}, bf16[256,2048]{1,0:T(8,128)(2,1)}, u32[]{:S(2)}, u32[]{:S(2)}) collective-permute-start(bf16[256,2048]{1,0:T(8,128)(2,1)S(1)} %copy-done.6), channel_id=1, source_target_pairs={{0,1},{1,0},{2,3},{3,2},{4,5},{5,4},{6,7},{7,6},{8,9},{9,8},{10,11... | collective-permute-start | bytes 3145736 | tf_op jit(solution)/shard_map/ppermute | solution.py:334
  40.5 50.6 %collective-permute-start.17 = (bf16[256,2048]{1,0:T(8,128)(2,1)S(1)}, bf16[256,2048]{1,0:T(8,128)(2,1)}, u32[]{:S(2)}, u32[]{:S(2)}) collective-permute-start(bf16[256,2048]{1,0:T(8,128)(2,1)S(1)} %collective-permute-done.13.refs_1_), channel_id=1, source_target_pairs={{0,1},{1,0},{2,3},{3,2},{4,5},{5,4},{6,7},{7,6},{8,9},{9,8},{10,11... | collective-permute-start | bytes 3145736 | tf_op jit(solution)/shard_map/ppermute | solution.py:334
  45.6 20.0 %copy-start.37 = (s32[8]{0:T(128)S(1)}, s32[8]{0:T(128)}, u32[]{:S(2)}) copy-start(s32[8]{0:T(128)} %param.18) | copy-start | bytes 100
  45.6 27.7 %copy-start.5 = (bf16[256,512]{1,0:T(8,128)(2,1)S(1)}, bf16[256,512]{1,0:T(8,128)(2,1)}, u32[]{:S(2)}) copy-start(bf16[256,512]{1,0:T(8,128)(2,1)} %refs_12_.3) | copy-start | bytes 786436
  45.6 76.8 %copy-start.34 = (s32[3]{0:T(128)S(1)}, s32[3]{0:T(128)}, u32[]{:S(2)}) copy-start(s32[3]{0:T(128)} %pad_add_fusion.2.where) | copy-start | bytes 40
  49.4 45.8 %all-to-all-start.3 = ((bf16[8,40,1024]{2,1,0:T(8,128)(2,1)}), bf16[8,40,1024]{2,1,0:T(8,128)(2,1)S(1)}, u32[]{:S(2)}, u32[]{:S(2)}) async-start(bf16[8,40,1024]{2,1,0:T(8,128)(2,1)} %prep.1), calls=%async_computation.3 | async-start | bytes 1310720 | tf_op jit(solution)/shard_map/all_to_all | solution.py:330
  64.1 31.1 %collective-permute-start.18 = (bf16[256,2048]{1,0:T(8,128)(2,1)}, bf16[256,2048]{1,0:T(8,128)(2,1)}, u32[]{:S(2)}, u32[]{:S(2)}) collective-permute-start(bf16[256,2048]{1,0:T(8,128)(2,1)} %collective-permute-done.14.refs_2_), channel_id=1, source_target_pairs={{0,1},{1,0},{2,3},{3,2},{4,5},{5,4},{6,7},{7,6},{8,9},{9,8},{10,11... | collective-permute-start | bytes 3145736 | tf_op jit(solution)/shard_map/ppermute | solution.py:334
  65.6 36.0 %collective-permute-start.19 = (bf16[256,2048]{1,0:T(8,128)(2,1)}, bf16[256,2048]{1,0:T(8,128)(2,1)}, u32[]{:S(2)}, u32[]{:S(2)}) collective-permute-start(bf16[256,2048]{1,0:T(8,128)(2,1)} %collective-permute-done.15.refs_3_), channel_id=1, source_target_pairs={{0,1},{1,0},{2,3},{3,2},{4,5},{5,4},{6,7},{7,6},{8,9},{9,8},{10,11... | collective-permute-start | bytes 3145736 | tf_op jit(solution)/shard_map/ppermute | solution.py:334
  65.6 4.1 %collective-permute-start.8 = (s32[8]{0:T(128)S(1)}, s32[8]{0:T(128)S(1)}, u32[]{:S(2)}, u32[]{:S(2)}) collective-permute-start(s32[8]{0:T(128)S(1)} %copy-done.37), channel_id=1, source_target_pairs={{0,1},{1,0},{2,3},{3,2},{4,5},{5,4},{6,7},{7,6},{8,9},{9,8},{10,11... | collective-permute-start | bytes 104 | tf_op jit(solution)/shard_map/ppermute | solution.py:334
  69.7 2.4 %collective-permute-start.11 = (s32[2,8]{1,0:T(2,128)S(1)}, s32[2,8]{1,0:T(2,128)S(1)}, u32[]{:S(2)}, u32[]{:S(2)}) collective-permute-start(s32[2,8]{1,0:T(2,128)S(1)} %get-tuple-element.36), channel_id=1, source_target_pairs={{0,6},{2,0},{4,2},{6,4},{1,7},{3,1},{5,3},{7,5},{8,14},{10,8},{12,... | collective-permute-start | bytes 200 | tf_op jit(solution)/shard_map/ppermute | solution.py:339
  72.1 4.2 %collective-permute-start.10 = (s32[2,8]{1,0:T(2,128)S(1)}, s32[2,8]{1,0:T(2,128)S(1)}, u32[]{:S(2)}, u32[]{:S(2)}) collective-permute-start(s32[2,8]{1,0:T(2,128)S(1)} %get-tuple-element.36), channel_id=1, source_target_pairs={{0,4},{2,6},{4,0},{6,2},{1,5},{3,7},{5,1},{7,3},{8,12},{10,14},{12... | collective-permute-start | bytes 200 | tf_op jit(solution)/shard_map/ppermute | solution.py:339
  76.4 3.6 %collective-permute-start.9 = (s32[2,8]{1,0:T(2,128)S(1)}, s32[2,8]{1,0:T(2,128)S(1)}, u32[]{:S(2)}, u32[]{:S(2)}) collective-permute-start(s32[2,8]{1,0:T(2,128)S(1)} %get-tuple-element.36), channel_id=1, source_target_pairs={{0,2},{2,4},{4,6},{6,0},{1,3},{3,5},{5,7},{7,1},{8,10},{10,12},{12... | collective-permute-start | bytes 200 | tf_op jit(solution)/shard_map/ppermute | solution.py:339
  80.0 7.9 %collective-permute-start.12 = (bf16[64,512]{1,0:T(8,128)(2,1)S(1)}, bf16[64,512]{1,0:T(8,128)(2,1)S(1)}, u32[]{:S(2)}, u32[]{:S(2)}) collective-permute-start(bf16[64,512]{1,0:T(8,128)(2,1)S(1)} %slice.17), channel_id=1, source_target_pairs={{8,0},{16,8},{24,16},{32,24},{40,32},{48,40},{56,48},{64,56},{72,6... | collective-permute-start | bytes 196616 | tf_op jit(solution)/shard_map/ppermute | solution.py:365
  88.5 15.2 %collective-permute-start.1 = (bf16[8,2,128,128]{3,2,1,0:T(8,128)(2,1)}, bf16[8,2,128,128]{3,2,1,0:T(8,128)(2,1)}, u32[]{:S(2)}, u32[]{:S(2)}) collective-permute-start(bf16[8,2,128,128]{3,2,1,0:T(8,128)(2,1)} %slice.16.kv), channel_id=1, source_target_pairs={{0,64},{64,128},{128,192},{1,65},{65,129},{129,193},{2,66},{66,130... | collective-permute-start | bytes 1572872 | tf_op jit(solution)/shard_map/ppermute | solution.py:344
  89.8 19.6 %collective-permute-start.3 = (bf16[8,2,128,128]{3,2,1,0:T(8,128)(2,1)}, bf16[8,2,128,128]{3,2,1,0:T(8,128)(2,1)}, u32[]{:S(2)}, u32[]{:S(2)}) collective-permute-start(bf16[8,2,128,128]{3,2,1,0:T(8,128)(2,1)} %slice.16.kv), channel_id=1, source_target_pairs={{0,128},{64,192},{1,129},{65,193},{2,130},{66,194},{3,131},{67,195... | collective-permute-start | bytes 1572872 | tf_op jit(solution)/shard_map/ppermute | solution.py:344
  91.1 28.6 %collective-permute-start.7 = (bf16[8,2,128,128]{3,2,1,0:T(8,128)(2,1)}, bf16[8,2,128,128]{3,2,1,0:T(8,128)(2,1)S(1)}, u32[]{:S(2)}, u32[]{:S(2)}) collective-permute-start(bf16[8,2,128,128]{3,2,1,0:T(8,128)(2,1)} %slice.16.kv), channel_id=1, source_target_pairs={{0,1},{1,0},{2,3},{3,2},{4,5},{5,4},{6,7},{7,6},{8,9},{9,8},{10,11... | collective-permute-start | bytes 1572872 | tf_op jit(solution)/shard_map/ppermute | solution.py:334
  95.1 33.4 %collective-permute-start.20 = (bf16[8,40,1024]{2,1,0:T(8,128)(2,1)S(1)}, bf16[8,40,1024]{2,1,0:T(8,128)(2,1)S(1)}, u32[]{:S(2)}, u32[]{:S(2)}) collective-permute-start(bf16[8,40,1024]{2,1,0:T(8,128)(2,1)S(1)} %all-to-all-done.3.e0.refs_8_), channel_id=1, source_target_pairs={{0,64},{64,128},{128,192},{192,0},{1,65},{65,129},{129,193},{193,1... | collective-permute-start | bytes 1966088 | tf_op jit(solution)/shard_map/ppermute | solution.py:339
  101.6 26.5 %collective-permute-start.5 = (bf16[8,2,128,128]{3,2,1,0:T(8,128)(2,1)}, bf16[8,2,128,128]{3,2,1,0:T(8,128)(2,1)}, u32[]{:S(2)}, u32[]{:S(2)}) collective-permute-start(bf16[8,2,128,128]{3,2,1,0:T(8,128)(2,1)} %slice.16.kv), channel_id=1, source_target_pairs={{0,192},{1,193},{2,194},{3,195},{4,196},{5,197},{6,198},{7,199},{8... | collective-permute-start | bytes 1572872 | tf_op jit(solution)/shard_map/ppermute | solution.py:344
  103.7 53.8 %collective-permute-start.2 = (bf16[8,2,128,128]{3,2,1,0:T(8,128)(2,1)}, bf16[8,2,128,128]{3,2,1,0:T(8,128)(2,1)}, u32[]{:S(2)}, u32[]{:S(2)}) collective-permute-start(bf16[8,2,128,128]{3,2,1,0:T(8,128)(2,1)} %collective-permute-done.1.kv1), channel_id=1, source_target_pairs={{0,1},{1,0},{2,3},{3,2},{4,5},{5,4},{6,7},{7,6},{8,9},{9,8},{10,11... | collective-permute-start | bytes 1572872 | tf_op jit(solution)/shard_map/ppermute | solution.py:334
  109.4 28.4 %collective-permute-start.21 = (bf16[8,40,1024]{2,1,0:T(8,128)(2,1)S(1)}, bf16[8,40,1024]{2,1,0:T(8,128)(2,1)S(1)}, u32[]{:S(2)}, u32[]{:S(2)}) collective-permute-start(bf16[8,40,1024]{2,1,0:T(8,128)(2,1)S(1)} %all-to-all-done.3.e0.refs_8_), channel_id=1, source_target_pairs={{0,128},{64,192},{128,0},{192,64},{1,129},{65,193},{129,1},{193,65... | collective-permute-start | bytes 1966088 | tf_op jit(solution)/shard_map/ppermute | solution.py:339
  120.6 28.5 %collective-permute-start.22 = (bf16[8,40,1024]{2,1,0:T(8,128)(2,1)S(1)}, bf16[8,40,1024]{2,1,0:T(8,128)(2,1)S(1)}, u32[]{:S(2)}, u32[]{:S(2)}) collective-permute-start(bf16[8,40,1024]{2,1,0:T(8,128)(2,1)S(1)} %all-to-all-done.3.e0.refs_8_), channel_id=1, source_target_pairs={{0,192},{64,0},{128,64},{192,128},{1,193},{65,1},{129,65},{193,129... | collective-permute-start | bytes 1966088 | tf_op jit(solution)/shard_map/ppermute | solution.py:339
  127.4 10.3 %copy-start.32 = (f32[8,8,128]{2,1,0:T(8,128)}, f32[8,8,128]{2,1,0:T(8,128)S(1)}, u32[]{:S(2)}) copy-start(f32[8,8,128]{2,1,0:T(8,128)S(1)} %get-tuple-element.23.l_i) | copy-start | bytes 98308
  128.0 30.4 %collective-permute-start.4 = (bf16[8,2,128,128]{3,2,1,0:T(8,128)(2,1)}, bf16[8,2,128,128]{3,2,1,0:T(8,128)(2,1)}, u32[]{:S(2)}, u32[]{:S(2)}) collective-permute-start(bf16[8,2,128,128]{3,2,1,0:T(8,128)(2,1)} %collective-permute-done.3.kv2), channel_id=1, source_target_pairs={{0,1},{1,0},{2,3},{3,2},{4,5},{5,4},{6,7},{7,6},{8,9},{9,8},{10,11... | collective-permute-start | bytes 1572872 | tf_op jit(solution)/shard_map/ppermute | solution.py:334
  128.5 30.0 %collective-permute-start.6 = (bf16[8,2,128,128]{3,2,1,0:T(8,128)(2,1)}, bf16[8,2,128,128]{3,2,1,0:T(8,128)(2,1)}, u32[]{:S(2)}, u32[]{:S(2)}) collective-permute-start(bf16[8,2,128,128]{3,2,1,0:T(8,128)(2,1)} %collective-permute-done.5.kv3), channel_id=1, source_target_pairs={{0,1},{1,0},{2,3},{3,2},{4,5},{5,4},{6,7},{7,6},{8,9},{9,8},{10,11... | collective-permute-start | bytes 1572872 | tf_op jit(solution)/shard_map/ppermute | solution.py:334
  131.2 17.8 %copy-start.26 = (bf16[256,128]{1,0:T(8,128)(2,1)S(1)}, bf16[256,128]{1,0:T(8,128)(2,1)}, u32[]{:S(2)}) copy-start(bf16[256,128]{1,0:T(8,128)(2,1)} %get-tuple-element.39.mem_v) | copy-start | bytes 196612
  131.2 17.8 %copy-start.27 = (bf16[256,128]{1,0:T(8,128)(2,1)S(1)}, bf16[256,128]{1,0:T(8,128)(2,1)}, u32[]{:S(2)}) copy-start(bf16[256,128]{1,0:T(8,128)(2,1)} %get-tuple-element.40.mem_k) | copy-start | bytes 196612
  131.2 17.8 %copy-start.35 = (f32[2048]{0:T(1024)S(1)}, f32[2048]{0:T(1024)}, u32[]{:S(2)}) copy-start(f32[2048]{0:T(1024)} %param.22) | copy-start | bytes 24580
  131.2 17.8 %copy-start.36 = (s32[4]{0:T(128)S(1)}, s32[4]{0:T(128)}, u32[]{:S(2)}) copy-start(s32[4]{0:T(128)} %off.3) | copy-start | bytes 52
  137.8 20.7 %copy-start.18 = (f32[8,128,128]{2,1,0:T(8,128)S(1)}, f32[8,128,128]{2,1,0:T(8,128)}, u32[]{:S(2)}) copy-start(f32[8,128,128]{2,1,0:T(8,128)} %copy-done.17) | copy-start | bytes 1572868
  137.8 20.7 %copy-start.31 = (f32[8,8,128]{2,1,0:T(8,128)S(1)}, f32[8,8,128]{2,1,0:T(8,128)}, u32[]{:S(2)}) copy-start(f32[8,8,128]{2,1,0:T(8,128)} %copy-done.30) | copy-start | bytes 98308
  137.8 20.7 %copy-start.33 = (f32[8,8,128]{2,1,0:T(8,128)S(1)}, f32[8,8,128]{2,1,0:T(8,128)}, u32[]{:S(2)}) copy-start(f32[8,8,128]{2,1,0:T(8,128)} %copy-done.32) | copy-start | bytes 98308
  155.8 27.8 %collective-permute-start.23 = (bf16[1024,128]{1,0:T(8,128)(2,1)S(1)}, bf16[1024,128]{1,0:T(8,128)(2,1)}, u32[]{:S(2)}, u32[]{:S(2)}) collective-permute-start(bf16[1024,128]{1,0:T(8,128)(2,1)S(1)} %encode.1.refs_0_), channel_id=1, source_target_pairs={{0,2},{2,4},{4,6},{6,0},{1,3},{3,5},{5,7},{7,1},{8,10},{10,12},{12... | collective-permute-start | bytes 786440 | tf_op jit(solution)/shard_map/ppermute | solution.py:339
  155.8 27.9 %collective-permute-start.24 = (bf16[1024,128]{1,0:T(8,128)(2,1)S(1)}, bf16[1024,128]{1,0:T(8,128)(2,1)}, u32[]{:S(2)}, u32[]{:S(2)}) collective-permute-start(bf16[1024,128]{1,0:T(8,128)(2,1)S(1)} %encode.1.refs_0_), channel_id=1, source_target_pairs={{0,4},{2,6},{4,0},{6,2},{1,5},{3,7},{5,1},{7,3},{8,12},{10,14},{12... | collective-permute-start | bytes 786440 | tf_op jit(solution)/shard_map/ppermute | solution.py:339
  157.5 26.6 %collective-permute-start.25 = (bf16[1024,128]{1,0:T(8,128)(2,1)S(1)}, bf16[1024,128]{1,0:T(8,128)(2,1)}, u32[]{:S(2)}, u32[]{:S(2)}) collective-permute-start(bf16[1024,128]{1,0:T(8,128)(2,1)S(1)} %encode.1.refs_0_), channel_id=1, source_target_pairs={{0,6},{2,0},{4,2},{6,4},{1,7},{3,1},{5,3},{7,5},{8,14},{10,8},{12,... | collective-permute-start | bytes 786440 | tf_op jit(solution)/shard_map/ppermute | solution.py:339
  177.8 21.7 %all-to-all-start.1 = ((bf16[8,128,128]{2,1,0:T(8,128)(2,1)}), bf16[8,128,128]{2,1,0:T(8,128)(2,1)}, u32[]{:S(2)}, u32[]{:S(2)}) async-start(bf16[8,128,128]{2,1,0:T(8,128)(2,1)} %copy-done.16), calls=%async_computation.1 | async-start | bytes 524288 | tf_op jit(solution)/shard_map/all_to_all | solution.py:330
  182.0 9.8 %collective-permute-start.26 = (bf16[1024,128]{1,0:T(8,128)(2,1)S(1)}, bf16[1024,128]{1,0:T(8,128)(2,1)S(1)}, u32[]{:S(2)}, u32[]{:S(2)}) collective-permute-start(bf16[1024,128]{1,0:T(8,128)(2,1)S(1)} %encode.1.refs_0_), channel_id=1, source_target_pairs={{0,1},{1,0},{2,3},{3,2},{4,5},{5,4},{6,7},{7,6},{8,9},{9,8},{10,11... | collective-permute-start | bytes 786440 | tf_op jit(solution)/shard_map/ppermute | solution.py:334
  183.6 8.2 %collective-permute-start.27 = (bf16[1024,128]{1,0:T(8,128)(2,1)}, bf16[1024,128]{1,0:T(8,128)(2,1)S(1)}, u32[]{:S(2)}, u32[]{:S(2)}) collective-permute-start(bf16[1024,128]{1,0:T(8,128)(2,1)} %collective-permute-done.23.refs_1_), channel_id=1, source_target_pairs={{0,1},{1,0},{2,3},{3,2},{4,5},{5,4},{6,7},{7,6},{8,9},{9,8},{10,11... | collective-permute-start | bytes 786440 | tf_op jit(solution)/shard_map/ppermute | solution.py:334
  183.7 8.1 %collective-permute-start.28 = (bf16[1024,128]{1,0:T(8,128)(2,1)}, bf16[1024,128]{1,0:T(8,128)(2,1)S(1)}, u32[]{:S(2)}, u32[]{:S(2)}) collective-permute-start(bf16[1024,128]{1,0:T(8,128)(2,1)} %collective-permute-done.24.refs_2_), channel_id=1, source_target_pairs={{0,1},{1,0},{2,3},{3,2},{4,5},{5,4},{6,7},{7,6},{8,9},{9,8},{10,11... | collective-permute-start | bytes 786440 | tf_op jit(solution)/shard_map/ppermute | solution.py:334
  184.1 7.7 %collective-permute-start.29 = (bf16[1024,128]{1,0:T(8,128)(2,1)}, bf16[1024,128]{1,0:T(8,128)(2,1)S(1)}, u32[]{:S(2)}, u32[]{:S(2)}) collective-permute-start(bf16[1024,128]{1,0:T(8,128)(2,1)} %collective-permute-done.25.refs_3_), channel_id=1, source_target_pairs={{0,1},{1,0},{2,3},{3,2},{4,5},{5,4},{6,7},{7,6},{8,9},{9,8},{10,11... | collective-permute-start | bytes 786440 | tf_op jit(solution)/shard_map/ppermute | solution.py:334
  196.2 20.0 %collective-permute-start.30 = (f32[64,512]{1,0:T(8,128)}, f32[64,512]{1,0:T(8,128)}, u32[]{:S(2)}, u32[]{:S(2)}) collective-permute-start(f32[64,512]{1,0:T(8,128)} %get-tuple-element.30), channel_id=1, source_target_pairs={{0,8},{8,16},{16,24},{24,32},{32,40},{40,48},{48,56},{56,64},{64,7... | collective-permute-start | bytes 393224 | tf_op jit(solution)/shard_map/ppermute | solution.py:400
  199.5 16.7 %all-to-all-start.2 = ((bf16[2,4,128,128]{3,2,1,0:T(8,128)(2,1)}), bf16[2,4,128,128]{3,2,1,0:T(8,128)(2,1)}, u32[]{:S(2)}, u32[]{:S(2)}) async-start(bf16[2,4,128,128]{3,2,1,0:T(8,128)(2,1)} %bitcast.4), calls=%async_computation.2 | async-start | bytes 524288 | tf_op jit(solution)/shard_map/all_to_all | solution.py:330
  (25 other events, 53.1 us)
where the time goes:
time: 219 us; the launch traced here: 218 us
  starting transfers between devices  81.3 us (37%)
  waiting for transfers between devices  51.9 us (24%)
  Pallas kernels  46.9 us (21%)
  local copies, waits for them, and re-layouts  27.5 us (13%)
  matrix products  7.5 us (3%)
  other arithmetic  2.66 us (1%)
    ppermute x12, waiting for transfers between devices, turn(): return lax.ppermute(a, axis, [(i, (i + distance) % n) for i in range(n)])  46.7 us
    ppermute x12, starting transfers between devices, turn(): return lax.ppermute(a, axis, [(i, (i + distance) % n) for i in range(n)])  26.9 us
    all_to_all x4, starting transfers between devices, swap(): return lax.all_to_all(a, axis, split_axis=0, concat_axis=0, tiled=True)  24 us
    unnamed x77, local copies, waits for them, and re-layouts  21.9 us
    pallas_call x1, Pallas kernels, far(): pl.pallas_call(far_kernel, out_shape=jax.ShapeDtypeStruct((8, 128, 128),...  18.6 us
    ppermute x14, starting transfers between devices, sibling(): return lax.ppermute(a, 'c', [(0, 1), (1, 0)])  18.3 us
    pallas_call x2, Pallas kernels, cross(): pl.pallas_call(body, out_shape=(o, o), grid=(1,), in_specs=[SMEM, kv_bloc...  8.17 us
    dot_general x1, matrix products, dot(): return jnp.dot(a, b, preferred_element_type=F32)  7.5 us
  transfers between devices with their start and end apart: 35, of which 8 were waited for; matrix products, arithmetic and copies ran while one was open for 8% of the time, Pallas kernels for 20%

commit v1 on v0

v1 whole, which is shorter than its diff:
```python
import jax
import jax.numpy as jnp
from jax import lax
from jax.experimental import pallas as pl
from jax.experimental.pallas import tpu as pltpu
from jax.sharding import Mesh, PartitionSpec as P


HD = 128
E = 2048
SPAN = 64
ROWS = 256
BLK = 16
DB_DEV = 16
LOG2E = 1.4426950408889634
SCALE = HD ** (-0.5)
MASKED = -1e30
BF = jnp.bfloat16
F32 = jnp.float32

VMEM = pl.BlockSpec(memory_space=pltpu.VMEM)
SMEM = pl.BlockSpec(memory_space=pltpu.SMEM)
ANY = pl.BlockSpec(memory_space=pl.ANY)


def dot(a, b):
    return jnp.dot(a, b, preferred_element_type=F32)


def dot_t(a, b):
    return lax.dot_general(a, b, (((1,), (1,)), ((), ())), preferred_element_type=F32)


def params(mib):
    return pltpu.CompilerParams(vmem_limit_bytes=mib << 20)


def pack_kernel(where, q, k, v, keep, send):
    c = where[2]
    for out, half in ((keep, c), (send, 1 - c)):
        rows = pl.ds(pl.multiple_of(half * 128, 128), 128)
        for j in range(4):
            cols = slice(j * 128, j * 128 + 128)
            out[j, 0] = q[rows, cols]
            out[j, 1] = k[rows, cols]
            out[j, 2] = v[rows, cols].T


def pack(where, q, k, v):
    o = jax.ShapeDtypeStruct((4, 3, 128, 128), BF)
    return pl.pallas_call(
        pack_kernel,
        out_shape=(o, o),
        in_specs=[SMEM] + [VMEM] * 3,
        out_specs=(VMEM, VMEM),
        name="pack",
    )(where, q, k, v)


def flash_step(keys, values, q, state, mask=None):
    s = dot_t(keys, q)
    if mask is not None:
        s = jnp.where(mask, s, MASKED)
    top = jnp.max(s, axis=0, keepdims=True)
    if state is None:
        new_max = top
    else:
        old_max, old_sum, acc = state
        new_max = jnp.maximum(old_max, top)
    p = jnp.exp2((s - new_max) * (SCALE * LOG2E))
    total = jnp.sum(p, axis=0, keepdims=True)
    out = dot(values, p.astype(BF))
    if state is None:
        return new_max, total, out
    shrink = jnp.exp2((old_max - new_max) * (SCALE * LOG2E))
    return new_max, old_sum * shrink + total, acc * shrink + out


def tiles(refs, places):
    keys = jnp.concatenate([ref[t, 0] for t in places for ref in refs], axis=0)
    values = jnp.concatenate([ref[t, 1] for t in places for ref in refs], axis=1)
    return keys, values


def near_kernel(where, q, kv, sib, state_o):
    c = where[2]
    row = lax.broadcasted_iota(jnp.int32, (256, 128), 0)
    col = lax.broadcasted_iota(jnp.int32, (256, 128), 1)
    mask = jnp.where(row < 128, (row <= col).astype(jnp.int32), c) > 0
    for z in range(8):
        state = flash_step(*tiles((kv, sib), (z,)), q[z], None, mask)
        for lo in range(0, z, 2):
            state = flash_step(*tiles((kv, sib), range(lo, min(lo + 2, z))), q[z], state)
        state_o[z, :128] = state[2]
        state_o[z, 128:136] = jnp.broadcast_to(state[0], (8, 128))
        state_o[z, 136:] = jnp.broadcast_to(state[1], (8, 128))


def near(where, q, kv, sib):
    return pl.pallas_call(
        near_kernel,
        out_shape=jax.ShapeDtypeStruct((8, 144, 128), F32),
        in_specs=[SMEM] + [VMEM] * 3,
        out_specs=VMEM,
        compiler_params=params(40),
        name="near",
    )(where, q, kv, sib)


def far_kernel(where, src, blk, q, *refs):
    kvs, state_i, blocks = refs[:6], refs[6], refs[7:15]
    out, x, state_s, kv_s, sib_s, sems = refs[15:]

    def fetch(i, carry):
        place, at = src[i], pl.multiple_of(blk[i] * BLK, BLK)

        def pick(lo, hi):
            if hi - lo == 1:
                pltpu.make_async_copy(
                    blocks[lo].at[pl.ds(at, BLK)],
                    x.at[pl.ds(pl.multiple_of(i * BLK, BLK), BLK)],
                    sems.at[i],
                ).start()
                return 0
            mid = (lo + hi) // 2
            return lax.cond(place < mid, lambda: pick(lo, mid), lambda: pick(mid, hi))

        return carry + pick(0, 8)

    lax.fori_loop(0, 64, fetch, 0)
    state_s[...] = state_i[...]

    def visit(r, carry):
        for i in range(3):
            kv, sib = kvs[2 * i : 2 * i + 2]

            @pl.when(r == i)
            def _(kv=kv, sib=sib):
                kv_s[...] = kv[...]
                sib_s[...] = sib[...]

        states = [
            (state_s[z, 128:129], state_s[z, 136:137], state_s[z, :128]) for z in range(8)
        ]
        for lo in (0, 4):
            keys, values = tiles((kv_s, sib_s), range(lo, lo + 4))
            states = [flash_step(keys, values, q[z], states[z]) for z in range(8)]
        for z in range(8):
            state_s[z, :128] = states[z][2]
            state_s[z, 128:136] = jnp.broadcast_to(states[z][0], (8, 128))
            state_s[z, 136:] = jnp.broadcast_to(states[z][1], (8, 128))
        return carry

    lax.fori_loop(0, where[0], visit, 0)
    for z in range(8):
        out[z] = (state_s[z, :128] / state_s[z, 136:137]).T.astype(BF)
    for i in range(64):
        rows = pl.ds(i * BLK, BLK)
        pltpu.make_async_copy(blocks[0].at[pl.ds(0, BLK)], x.at[rows], sems.at[i]).wait()


def far(where, src, blk, q, pairs, state, blocks):
    return pl.pallas_call(
        far_kernel,
        out_shape=(
            jax.ShapeDtypeStruct((8, 128, 128), BF),
            jax.ShapeDtypeStruct((1024, E), BF),
        ),
        in_specs=[SMEM] * 3 + [VMEM] * 8 + [pl.BlockSpec(memory_space=pltpu.HBM)] * 8,
        out_specs=(VMEM, pl.BlockSpec(memory_space=pltpu.HBM)),
        scratch_shapes=[
            pltpu.VMEM((8, 144, 128), F32),
            pltpu.VMEM((8, 2, 128, 128), BF),
            pltpu.VMEM((8, 2, 128, 128), BF),
            pltpu.SemaphoreType.DMA((64,)),
        ],
        compiler_params=params(20),
        name="far",
    )(where, src, blk, q, *pairs, state, *blocks)


def prep_kernel(enc_out, weight, encq, out):
    w2 = dot(enc_out[...], weight[...]).astype(BF)
    eq = jnp.concatenate([encq[j * 8 : j * 8 + 8] for j in range(8)], axis=1)
    for z in range(8):
        out[z, :32] = w2
        out[z, 32:] = eq


def prep(enc_out, weight, encq):
    return pl.pallas_call(
        prep_kernel,
        out_shape=jax.ShapeDtypeStruct((8, 40, 1024), BF),
        in_specs=[VMEM] * 3,
        out_specs=VMEM,
        compiler_params=params(24),
        name="prep",
    )(enc_out, weight, encq)


def encode_kernel(off, where, x_hbm, e0, e1, e2, e3, gain, mem_k, mem_v, ctx, encq, x, sems):
    def piece_of(span):
        rows = pl.ds(pl.multiple_of(span * ROWS, ROWS), ROWS)
        return pltpu.make_async_copy(x_hbm.at[rows], x.at[rows], sems.at[span])

    for span in range(4):
        piece_of(span).start()
    y = where[0]
    for r, ref in enumerate((e0, e1, e2, e3)):
        for z in range(8):
            for j in range(8):
                piece = ref[z, :, j * 128 : j * 128 + 128]
                encq[lax.rem(y + 4 - r, 4), z * 64 + j * 8 : z * 64 + j * 8 + 8] = piece

    def encode_span(span, carry):
        piece_of(span).wait()
        rows = pl.ds(pl.multiple_of(span * ROWS, ROWS), ROWS)
        wide = x[rows].astype(F32)
        mean = jnp.mean(wide * wide, axis=1, keepdims=True)
        h = (wide * lax.rsqrt(mean + 1e-6) * gain[...]).astype(BF)
        eq = (dot(h, encq[...].reshape(E, HD)) * SCALE).astype(BF)
        tokens = pl.ds(pl.multiple_of(span * SPAN, SPAN), SPAN)
        s = dot_t(eq, mem_k[tokens])
        seen = lax.broadcasted_iota(jnp.int32, (ROWS, SPAN), 1) < off[span]
        s = jnp.where(seen, s, MASKED)
        top = jnp.max(s, axis=1, keepdims=True)
        p = jnp.where(seen, jnp.exp(s - top), 0.0)
        total = jnp.sum(p, axis=1, keepdims=True)
        ctx[rows] = (dot(p.astype(BF), mem_v[tokens]) / total).astype(BF)
        return carry

    lax.fori_loop(0, 4, encode_span, 0)


def encode(off, where, x, encqs, gain, mem_k, mem_v):
    return pl.pallas_call(
        encode_kernel,
        out_shape=jax.ShapeDtypeStruct((1024, 128), BF),
        in_specs=[SMEM] * 2 + [pl.BlockSpec(memory_space=pltpu.HBM)] + [VMEM] * 7,
        out_specs=VMEM,
        scratch_shapes=[
            pltpu.VMEM((4, 512, 128), BF),
            pltpu.VMEM((1024, E), BF),
            pltpu.SemaphoreType.DMA((4,)),
        ],
        compiler_params=params(20),
        name="encode",
    )(off, where, x, *encqs, gain, mem_k, mem_v)


def attend(q, keys, values):
    s = dot_t(q, keys) * (SCALE * LOG2E)
    p = jnp.exp2(s - jnp.max(s, axis=1, keepdims=True))
    return dot(p.astype(BF), values) / jnp.sum(p, axis=1, keepdims=True)


def cross_kernel(off, where, kvx, *refs):
    ctx, w2s, (q, qn, cca_o, rem_o, w2, ear) = refs[:8], refs[8:12], refs[12:]
    y, x, c = where[0], where[1], where[2]
    for turned in range(4):
        r = lax.rem(x - y + turned + 4, 4)
        for side, cc in ((0, c), (1, 1 - c)):
            for z in range(4):
                w2[side, r, z * 32 : z * 32 + 32] = w2s[turned][4 * cc + z]
    pos = lax.broadcasted_iota(jnp.int32, (SPAN, HD), 0)

    def cross_span(span, carry):
        rows = pl.ds(pl.multiple_of(span * ROWS, ROWS), ROWS)
        context = jnp.concatenate([ref[rows] for ref in ctx], axis=1)
        kv = (kvx[rows] + dot(context, w2[...].reshape(1024, 1024))).astype(BF)
        at = pl.ds(pl.multiple_of(span * SPAN, SPAN), SPAN)
        after_at = pl.ds(pl.multiple_of(jnp.minimum(span + 1, 3) * SPAN, SPAN), SPAN)
        later = jnp.where(span == 3, qn[...], q[after_at])
        both = jnp.concatenate([q[at], later], axis=0)
        own_seen = (pos >= off[span]) | (span == 0)
        for j in range(4):
            cols = slice(j * 128, j * 128 + 128)
            out = attend(both[:, cols], kv[:, cols], kv[:, 512 + j * 128 : 640 + j * 128])
            cca_o[at, cols] = jnp.where(own_seen, out[:SPAN], ear[:, cols])
            ear[:, cols] = out[SPAN:]
        return carry

    ear[...] = jnp.zeros((SPAN, 512), F32)
    lax.fori_loop(0, 4, cross_span, 0)
    rem_o[...] = ear[...]


def cross(off, where, kvx, ctx, w2s, q, qn):
    return pl.pallas_call(
        cross_kernel,
        out_shape=(
            jax.ShapeDtypeStruct((256, 512), F32),
            jax.ShapeDtypeStruct((SPAN, 512), F32),
        ),
        in_specs=[SMEM] * 2 + [VMEM] * 15,
        out_specs=(VMEM, VMEM),
        scratch_shapes=[pltpu.VMEM((2, 4, 128, 1024), BF), pltpu.VMEM((SPAN, 512), F32)],
        compiler_params=params(20),
        name="cross",
    )(off, where, kvx, *ctx, *w2s, q, qn)


def final_kernel(off, attn, cca, recv, out):
    pos = lax.broadcasted_iota(jnp.int32, (SPAN, 512), 0)
    for span in range(4):
        at = slice(span * SPAN, span * SPAN + SPAN)
        add = cca[at]
        if span == 0:
            add = jnp.where(pos >= off[0], add, recv[...])
        rows = slice((span % 2) * SPAN, (span % 2) * SPAN + SPAN)
        self_out = jnp.concatenate([attn[span // 2, j, rows] for j in range(4)], axis=1)
        out[at] = (self_out.astype(F32) + add).astype(BF)


def final(off, attn, cca, recv):
    return pl.pallas_call(
        final_kernel,
        out_shape=jax.ShapeDtypeStruct((256, 512), BF),
        in_specs=[SMEM] + [VMEM] * 3,
        out_specs=VMEM,
        name="final",
    )(off, attn, cca, recv)


def swap(a, axis):
    return lax.all_to_all(a, axis, split_axis=0, concat_axis=0, tiled=True)


def sibling(a):
    return lax.ppermute(a, "c", [(0, 1), (1, 0)])


def turn(a, axis, distance):
    n = lax.axis_size(axis)
    return lax.ppermute(a, axis, [(i, (i + distance) % n) for i in range(n)])


def onward(a, axis, distance):
    n = lax.axis_size(axis)
    return lax.ppermute(a, axis, [(i, i + distance) for i in range(n - distance)])


def block(
    q_self, k_self, v_self, q_cca, memory, database, nbr_block, span_offset,
    enc_query, enc_out, enc_gain, cca_kv,
):
    y, x, c = lax.axis_index("y"), lax.axis_index("x"), lax.axis_index("c")
    where = jnp.stack([y, x, c]).astype(jnp.int32)
    nb = 2 * x + c
    steps = lax.axis_size("y") * lax.axis_size("z")

    pair = jnp.stack([nbr_block, sibling(nbr_block)])
    keep, send = pack(where, q_self, k_self, v_self)
    send = sibling(send)
    first, second = jnp.where(c == 0, keep, send), jnp.where(c == 0, send, keep)
    qkv = jnp.concatenate([first, second])
    pairs = jnp.stack([pair] + [turn(pair, "x", r) for r in (1, 2, 3)])
    cca_kv, pairs = lax.optimization_barrier((cca_kv, pairs))
    blocks = [database] + [turn(database, "x", r) for r in (1, 2, 3)]
    blocks = blocks + [sibling(database)]
    blocks = blocks + [sibling(b) for b in blocks[1:4]]
    qn = lax.ppermute(q_cca[:SPAN], ("y", "z"), [(i, i - 1) for i in range(1, steps)])

    qkv = swap(qkv, "z")
    weight = cca_kv.reshape(E, 1024)
    encq = lax.dynamic_slice(enc_query, (0, nb * HD), (64, HD))
    bundle = prep(enc_out, weight, encq)
    qkv, bundle = lax.optimization_barrier((qkv, bundle))
    q, kv = qkv[:, 0], qkv[:, 1:]
    kvs = [kv] + [onward(kv, "y", r) for r in (1, 2, 3)]
    sibs = [sibling(kv)]
    sibs = sibs + [sibling(a) for a in kvs[1:]]

    bundle = swap(bundle, "z")
    near_out = near(where, q, kv, sibs[0])
    pairs, _ = lax.optimization_barrier((pairs, near_out))
    ours = jnp.arange(4, dtype=jnp.int32)
    ids = pairs[(x - ours) % 4]
    ids = jnp.where(c == 0, ids, ids[:, ::-1]).reshape(-1)
    owner = ids // DB_DEV
    slot = (ids % DB_DEV).astype(jnp.int32)
    src = ((x - owner // 2) % 4 + 4 * (owner % 2 != c)).astype(jnp.int32)
    mem = lax.dynamic_slice(memory, (0, 0, nb * HD), (256, 2, HD))
    mem_k, mem_v = mem[:, 0], mem[:, 1]
    bundle, src, slot, mem_k, mem_v = lax.optimization_barrier((bundle, src, slot, mem_k, mem_v))
    encq, w2 = bundle[:, 32:], bundle[:, :32]
    encqs = [encq] + [turn(encq, "y", r) for r in (1, 2, 3)]
    w2s = [w2] + [turn(w2, "y", r) for r in (1, 2, 3)]

    halves = [a for r in (1, 2, 3) for a in (kvs[r], sibs[r])]
    attn, rows = far(where, src, slot, q, halves, near_out, blocks)
    ctx = encode(
        span_offset, where, rows, encqs, enc_gain.reshape(1, E), mem_k, mem_v
    )
    qn, ctx = lax.optimization_barrier((qn, ctx))
    kvx = dot(rows, weight)
    ctxs = [ctx] + [turn(ctx, "x", r) for r in (1, 2, 3)]
    ctxs = ctxs + [sibling(ctx)]
    ctxs = ctxs + [sibling(a) for a in ctxs[1:4]]
    back = swap(attn, "z").reshape(2, 4, 128, 128)
    cca, rem = cross(span_offset, where, kvx, ctxs, w2s, q_cca, qn)
    recv = lax.ppermute(rem, ("y", "z"), [(i, i + 1) for i in range(steps - 1)])
    back = swap(back, "c")
    return final(span_offset, back, cca, recv)


def solution(mesh):
    fine = Mesh(mesh.devices.reshape(4, 8, 4, 2), ("y", "z", "x", "c"))
    s, n = ("y", "z"), ("x", "c")
    in_specs = (
        P(s, n), P(s, n), P(s, n), P(s, n),
        P(s, None, None),
        P((*s, *n), None),
        P((*s, *n)),
        P(s),
        P(s, None),
        P(s, None),
        P(),
        P(None, None, n),
    )
    return jax.shard_map(block, mesh=fine, in_specs=in_specs, out_specs=P(s, n), check_vma=False)
```

time: 219 us -> 209 us (0.954)
  the two profiles are of different devices: /device:TPU:25 before, /device:TPU:1 now
where the time goes in v1:
time: 209 us; the launch traced here: 208 us
  waiting for transfers between devices  79.8 us (38%)
  starting transfers between devices  70.2 us (34%)
  Pallas kernels  24.6 us (12%)
  local copies, waits for them, and re-layouts  15.9 us (8%)
  matrix products  7.51 us (4%)
  blocking collectives  7.13 us (3%)
  other arithmetic  2.69 us (1%)
    ppermute x15, waiting for transfers between devices, turn(): return lax.ppermute(a, axis, [(i, (i + distance) % n) for i in range(n)])  62 us
    ppermute x15, starting transfers between devices, turn(): return lax.ppermute(a, axis, [(i, (i + distance) % n) for i in range(n)])  22.4 us
    all_to_all x3, starting transfers between devices, swap(): return lax.all_to_all(a, axis, split_axis=0, concat_axis=0, tiled=True)  17.5 us
    ppermute x14, starting transfers between devices, sibling(): return lax.ppermute(a, 'c', [(0, 1), (1, 0)])  16.1 us
    ppermute x3, waiting for transfers between devices, onward(): lax.ppermute(a, axis, [(i, i + distance) for i in range(n - distance)])  13.6 us
    unnamed x37, local copies, waits for them, and re-layouts  10.9 us
    ppermute x3, starting transfers between devices, onward(): lax.ppermute(a, axis, [(i, i + distance) for i in range(n - distance)])  9.88 us
    dot_general x1, matrix products, dot(): return jnp.dot(a, b, preferred_element_type=F32)  7.51 us
  transfers between devices with their start and end apart: 37, of which 12 were waited for; matrix products, arithmetic and copies ran while one was open for 9% of the time, Pallas kernels for 10%

profile of v1, /device:TPU:1, one launch (start us, length us, event | category | flops | bytes accessed | tf_op | source)
XLA Modules:
  0.0 208.2 jit_solution(3293381719156847075)
XLA Ops:
  0.6 2.1 %pack.1 = (bf16[4,3,128,128]{3,2,1,0:T(8,128)(2,1)}, bf16[4,3,128,128]{3,2,1,0:T(8,128)(2,1)}) custom-call(s32[3]{0:T(128)} %pad_add_fusion.2.where, bf16[256,512]{1,0:T(8,128)(2,1)} %q.1, bf16[256,512]{1,0:T(8,128)(2,1)} %k.1, bf16[256,512]{1,0:T(8,128)(2,1)} %v.1), custom_call_target="tpu_custom_call" | custom-call | tf_op jit(solution)/shard_map/pack/pallas_call | solution.py:51
  2.8 3.2 %collective-permute-start = (bf16[4,3,128,128]{3,2,1,0:T(8,128)(2,1)}, bf16[4,3,128,128]{3,2,1,0:T(8,128)(2,1)S(1)}, u32[]{:S(2)}, u32[]{:S(2)}) collective-permute-start(bf16[4,3,128,128]{3,2,1,0:T(8,128)(2,1)} %get-tuple-element.24), channel_id=1, source_target_pairs={{0,1},{1,0},{2,3},{3,2},{4,5},{5,4},{6,7},{7,6},{8,9},{9,8},{10,11... | collective-permute-start | bytes 1179656 | tf_op jit(solution)/shard_map/ppermute | solution.py:330
  6.0 1.6 collective-permute-done
  7.5 1.1 broadcast_select_fusion.1
  9.5 6.5 %all-to-all-start = ((bf16[8,3,128,128]{3,2,1,0:T(8,128)(2,1)}), bf16[8,3,128,128]{3,2,1,0:T(8,128)(2,1)S(1)}, u32[]{:S(2)}, u32[]{:S(2)}) async-start(bf16[8,3,128,128]{3,2,1,0:T(8,128)(2,1)} %pad_maximum_fusion), calls=%async_computation | async-start | bytes 1572864 | tf_op jit(solution)/shard_map/all_to_all | solution.py:326
  16.0 2.8 %collective-permute-start.13 = (bf16[256,2048]{1,0:T(8,128)(2,1)S(1)}, bf16[256,2048]{1,0:T(8,128)(2,1)}, u32[]{:S(2)}, u32[]{:S(2)}) collective-permute-start(bf16[256,2048]{1,0:T(8,128)(2,1)S(1)} %copy-done.3), channel_id=1, source_target_pairs={{0,4},{2,6},{4,0},{6,2},{1,5},{3,7},{5,1},{7,3},{8,12},{10,14},{12... | collective-permute-start | bytes 3145736 | tf_op jit(solution)/shard_map/ppermute | solution.py:335
  19.7 1.2 collective-permute-start.15
  20.9 33.7 %collective-permute-done.12.refs_8_ = bf16[256,2048]{1,0:T(8,128)(2,1)} collective-permute-done((bf16[256,2048]{1,0:T(8,128)(2,1)}, bf16[256,2048]{1,0:T(8,128)(2,1)}, u32[]{:S(2)}, u32[]{:S(2)}) %collective-permute-start.12) | collective-permute-done | bytes 1048608 | tf_op jit(solution)/shard_map/ppermute | solution.py:335
  55.5 2.6 %collective-permute-done.1 = s32[8]{0:T(128)S(1)} collective-permute-done((s32[8]{0:T(128)S(1)}, s32[8]{0:T(128)S(1)}, u32[]{:S(2)}, u32[]{:S(2)}) %collective-permute-start.1) | collective-permute-done | bytes 64 | tf_op jit(solution)/shard_map/ppermute | solution.py:330
  58.2 3.6 %collective-permute-done.2 = s32[2,8]{1,0:T(2,128)S(1)} collective-permute-done((s32[2,8]{1,0:T(2,128)S(1)}, s32[2,8]{1,0:T(2,128)S(1)}, u32[]{:S(2)}, u32[]{:S(2)}) %collective-permute-start.2) | collective-permute-done | bytes 96 | tf_op jit(solution)/shard_map/ppermute | solution.py:335
  61.8 3.9 %collective-permute-done.3 = s32[2,8]{1,0:T(2,128)S(1)} collective-permute-done((s32[2,8]{1,0:T(2,128)S(1)}, s32[2,8]{1,0:T(2,128)S(1)}, u32[]{:S(2)}, u32[]{:S(2)}) %collective-permute-start.3) | collective-permute-done | bytes 96 | tf_op jit(solution)/shard_map/ppermute | solution.py:335
  66.4 1.8 collective-permute-done.4
  68.2 3.4 %copy.17 = bf16[256,8,2,512]{3,1,2,0:T(8,128)(2,1)S(1)} copy(bf16[256,8,2,512]{3,2,1,0:T(2,128)(2,1)} %bitcast.30) | data formatting | bytes 8388608
  71.6 1.7 prep.1
  73.3 2.0 copy-done.1
  76.2 4.0 %collective-permute-start.5 = (bf16[8,2,128,128]{3,2,1,0:T(8,128)(2,1)S(1)}, bf16[8,2,128,128]{3,2,1,0:T(8,128)(2,1)S(1)}, u32[]{:S(2)}, u32[]{:S(2)}) collective-permute-start(bf16[8,2,128,128]{3,2,1,0:T(8,128)(2,1)S(1)} %slice.22.kv), channel_id=1, source_target_pairs={{0,1},{1,0},{2,3},{3,2},{4,5},{5,4},{6,7},{7,6},{8,9},{9,8},{10,11... | collective-permute-start | bytes 1572872 | tf_op jit(solution)/shard_map/ppermute | solution.py:330
  80.2 4.3 %all-to-all-start.1 = ((bf16[8,40,1024]{2,1,0:T(8,128)(2,1)}), bf16[8,40,1024]{2,1,0:T(8,128)(2,1)}, u32[]{:S(2)}, u32[]{:S(2)}) async-start(bf16[8,40,1024]{2,1,0:T(8,128)(2,1)} %prep.1), calls=%async_computation.1 | async-start | bytes 1310720 | tf_op jit(solution)/shard_map/all_to_all | solution.py:326
  84.5 1.3 constant_dynamic-slice_fusion.1
  86.5 5.4 %collective-permute-start.10 = (bf16[8,2,128,128]{3,2,1,0:T(8,128)(2,1)S(1)}, bf16[8,2,128,128]{3,2,1,0:T(8,128)(2,1)}, u32[]{:S(2)}, u32[]{:S(2)}) collective-permute-start(bf16[8,2,128,128]{3,2,1,0:T(8,128)(2,1)S(1)} %slice.22.kv), channel_id=1, source_target_pairs={{0,192},{1,193},{2,194},{3,195},{4,196},{5,197},{6,198},{7,199},{8... | collective-permute-start | bytes 1572872 | tf_op jit(solution)/shard_map/ppermute | solution.py:340
  91.9 2.1 %collective-permute-start.6 = (bf16[8,2,128,128]{3,2,1,0:T(8,128)(2,1)S(1)}, bf16[8,2,128,128]{3,2,1,0:T(8,128)(2,1)}, u32[]{:S(2)}, u32[]{:S(2)}) collective-permute-start(bf16[8,2,128,128]{3,2,1,0:T(8,128)(2,1)S(1)} %slice.22.kv), channel_id=1, source_target_pairs={{0,64},{64,128},{128,192},{1,65},{65,129},{129,193},{2,66},{66,130... | collective-permute-start | bytes 1572872 | tf_op jit(solution)/shard_map/ppermute | solution.py:340
  94.0 2.4 %collective-permute-start.8 = (bf16[8,2,128,128]{3,2,1,0:T(8,128)(2,1)S(1)}, bf16[8,2,128,128]{3,2,1,0:T(8,128)(2,1)}, u32[]{:S(2)}, u32[]{:S(2)}) collective-permute-start(bf16[8,2,128,128]{3,2,1,0:T(8,128)(2,1)S(1)} %slice.22.kv), channel_id=1, source_target_pairs={{0,128},{64,192},{1,129},{65,193},{2,130},{66,194},{3,131},{67,195... | collective-permute-start | bytes 1572872 | tf_op jit(solution)/shard_map/ppermute | solution.py:340
  96.4 1.0 slice_bitcast_fusion.q
  97.4 2.6 %near.1.refs_6_ = f32[8,144,128]{2,1,0:T(8,128)S(1)} custom-call(s32[3]{0:T(128)S(1)} %copy-done.12, bf16[8,128,128]{2,1,0:T(8,128)(2,1)S(1)} %slice_bitcast_fusion.q, bf16[8,2,128,128]{3,2,1,0:T(8,128)(2,1)S(1)} %slice.22.kv, bf16[8,2,128,128]{3,2,1,0:T(8,128)(2,1)S(1)} %collective-permute-done.5.sib), custom_call_target="tpu_custom_call" | custom-call | tf_op jit(solution)/shard_map/near/pallas_call | solution.py:100
  100.6 12.7 %collective-permute-done.10.refs_4_ = bf16[8,2,128,128]{3,2,1,0:T(8,128)(2,1)} collective-permute-done((bf16[8,2,128,128]{3,2,1,0:T(8,128)(2,1)S(1)}, bf16[8,2,128,128]{3,2,1,0:T(8,128)(2,1)}, u32[]{:S(2)}, u32[]{:S(2)}) %collective-permute-start.10) | collective-permute-done | bytes 524320 | tf_op jit(solution)/shard_map/ppermute | solution.py:340
  113.3 1.2 collective-permute-start.11
  115.4 1.2 collective-permute-start.9
  116.7 1.1 slice.27.refs_8_
  118.8 3.6 %collective-permute-start.20 = (bf16[8,8,1024]{2,1,0:T(8,128)(2,1)S(1)}, bf16[8,8,1024]{2,1,0:T(8,128)(2,1)S(1)}, u32[]{:S(2)}, u32[]{:S(2)}) collective-permute-start(bf16[8,8,1024]{2,1,0:T(8,128)(2,1)S(1)} %slice.26.e0), channel_id=1, source_target_pairs={{0,64},{64,128},{128,192},{192,0},{1,65},{65,129},{129,193},{193,1... | collective-permute-start | bytes 393224 | tf_op jit(solution)/shard_map/ppermute | solution.py:335
  122.8 2.1 collective-permute-start.22
  124.9 1.3 collective-permute-start.19
  126.2 5.7 %far.1 = (bf16[8,128,128]{2,1,0:T(8,128)(2,1)S(1)}, bf16[1024,2048]{1,0:T(8,128)(2,1)S(1)}) custom-call(s32[3]{0:T(128)S(1)} %copy-done.12, s32[64]{0:T(128)S(1)} %get-tuple-element.30.src, s32[64]{0:T(128)S(1)} %get-tuple-element.31.blk, bf16[8,128,128]{2,1,0:T(8,128)(2,1)S(1)} %slice_bitcast_fusion.q, ...), custom_call_target="tpu_custom_call" | custom-call | tf_op jit(solution)/shard_map/far/pallas_call | solution.py:163
  131.9 3.4 %collective-permute-done.20.e1 = bf16[8,8,1024]{2,1,0:T(8,128)(2,1)S(1)} collective-permute-done((bf16[8,8,1024]{2,1,0:T(8,128)(2,1)S(1)}, bf16[8,8,1024]{2,1,0:T(8,128)(2,1)S(1)}, u32[]{:S(2)}, u32[]{:S(2)}) %collective-permute-start.20) | collective-permute-done | bytes 131104 | tf_op jit(solution)/shard_map/ppermute | solution.py:335
  135.4 4.2 %collective-permute-done.21.e2 = bf16[8,8,1024]{2,1,0:T(8,128)(2,1)S(1)} collective-permute-done((bf16[8,8,1024]{2,1,0:T(8,128)(2,1)S(1)}, bf16[8,8,1024]{2,1,0:T(8,128)(2,1)S(1)}, u32[]{:S(2)}, u32[]{:S(2)}) %collective-permute-start.21) | collective-permute-done | bytes 131104 | tf_op jit(solution)/shard_map/ppermute | solution.py:335
  139.6 5.0 %encode.1.refs_0_ = bf16[1024,128]{1,0:T(8,128)(2,1)S(1)} custom-call(s32[4]{0:T(128)S(1)} %copy-done.14, s32[3]{0:T(128)S(1)} %copy-done.12, bf16[1024,2048]{1,0:T(8,128)(2,1)S(1)} %get-tuple-element.33.x_hbm, bf16[8,8,1024]{2,1,0:T(8,128)(2,1)S(1)} %slice.26.e0, bf16[8,8,1024]{2,1,0:T(8,128)(2,1)S(1)} %collective-permute-done.20.e1, ...), custom_call_target="tpu_custom_call" | custom-call | tf_op jit(solution)/shard_map/encode/pallas_call | solution.py:236
  144.6 2.0 copy-done.2
  147.4 3.7 %collective-permute-start.24 = (bf16[1024,128]{1,0:T(8,128)(2,1)S(1)}, bf16[1024,128]{1,0:T(8,128)(2,1)S(1)}, u32[]{:S(2)}, u32[]{:S(2)}) collective-permute-start(bf16[1024,128]{1,0:T(8,128)(2,1)S(1)} %encode.1.refs_0_), channel_id=1, source_target_pairs={{0,4},{2,6},{4,0},{6,2},{1,5},{3,7},{5,1},{7,3},{8,12},{10,14},{12... | collective-permute-start | bytes 786440 | tf_op jit(solution)/shard_map/ppermute | solution.py:335
  151.0 1.1 collective-permute-start.26
  152.2 6.8 %all-to-all-start.2 = ((bf16[8,128,128]{2,1,0:T(8,128)(2,1)}), bf16[8,128,128]{2,1,0:T(8,128)(2,1)}, u32[]{:S(2)}, u32[]{:S(2)}) async-start(bf16[8,128,128]{2,1,0:T(8,128)(2,1)} %copy-done.10), calls=%async_computation.2 | async-start | bytes 524288 | tf_op jit(solution)/shard_map/all_to_all | solution.py:326
  158.9 1.6 collective-permute-start.31
  160.5 2.0 collective-permute-done.24.refs_2_
  162.5 5.9 %collective-permute-start.32 = (bf16[8,32,1024]{2,1,0:T(8,128)(2,1)S(1)}, bf16[8,32,1024]{2,1,0:T(8,128)(2,1)S(1)}, u32[]{:S(2)}, u32[]{:S(2)}) collective-permute-start(bf16[8,32,1024]{2,1,0:T(8,128)(2,1)S(1)} %slice.27.refs_8_), channel_id=1, source_target_pairs={{0,192},{64,0},{128,64},{192,128},{1,193},{65,1},{129,65},{193,129... | collective-permute-start | bytes 1572872 | tf_op jit(solution)/shard_map/ppermute | solution.py:335
  168.4 2.2 %collective-permute-start.27 = (bf16[1024,128]{1,0:T(8,128)(2,1)S(1)}, bf16[1024,128]{1,0:T(8,128)(2,1)S(1)}, u32[]{:S(2)}, u32[]{:S(2)}) collective-permute-start(bf16[1024,128]{1,0:T(8,128)(2,1)S(1)} %collective-permute-done.23.refs_1_), channel_id=1, source_target_pairs={{0,1},{1,0},{2,3},{3,2},{4,5},{5,4},{6,7},{7,6},{8,9},{9,8},{10,11... | collective-permute-start | bytes 786440 | tf_op jit(solution)/shard_map/ppermute | solution.py:330
  171.1 7.5 %fusion.5.kvx = f32[1024,1024]{1,0:T(8,128)S(1)} fusion(bf16[1024,2048]{1,0:T(8,128)(2,1)} %copy-done.2, bf16[2048,1024]{1,0:T(8,128)(2,1)} %bitcast.28), kind=kOutput, calls=%fused_computation.38 | convolution fusion | flops 4294967296 | bytes 12582912 | tf_op jit(solution)/shard_map/dot_general | solution.py:27
  178.6 9.3 %collective-permute-done.32.refs_11_ = bf16[8,32,1024]{2,1,0:T(8,128)(2,1)S(1)} collective-permute-done((bf16[8,32,1024]{2,1,0:T(8,128)(2,1)S(1)}, bf16[8,32,1024]{2,1,0:T(8,128)(2,1)S(1)}, u32[]{:S(2)}, u32[]{:S(2)}) %collective-permute-start.32) | collective-permute-done | bytes 524320 | tf_op jit(solution)/shard_map/ppermute | solution.py:335
  189.9 5.5 %cross.1 = (f32[256,512]{1,0:T(8,128)S(1)}, f32[64,512]{1,0:T(8,128)S(1)}) custom-call(s32[4]{0:T(128)S(1)} %copy-done.14, s32[3]{0:T(128)S(1)} %copy-done.12, f32[1024,1024]{1,0:T(8,128)S(1)} %fusion.5.kvx, bf16[1024,128]{1,0:T(8,128)(2,1)S(1)} %encode.1.refs_0_, bf16[1024,128]{1,0:T(8,128)(2,1)S(1)} %copy-done.7, bf16[1024,128]{1,0:T(8,128)(2,1)S(1)} %copy-done.9, ...), custom_call_target="tpu_custom_call" | custom-call | tf_op jit(solution)/shard_map/cross/pallas_call | solution.py:289
  195.4 3.1 %collective-permute-start.33 = (f32[64,512]{1,0:T(8,128)S(1)}, f32[64,512]{1,0:T(8,128)S(1)}, u32[]{:S(2)}, u32[]{:S(2)}) collective-permute-start(f32[64,512]{1,0:T(8,128)S(1)} %get-tuple-element.40), channel_id=1, source_target_pairs={{0,8},{8,16},{16,24},{24,32},{32,40},{40,48},{48,56},{56,64},{64,7... | collective-permute-start | bytes 393224 | tf_op jit(solution)/shard_map/ppermute | solution.py:402
  198.5 7.1 %all_to_all.20.attn = bf16[2,4,128,128]{3,2,1,0:T(8,128)(2,1)} all-to-all(bf16[2,4,128,128]{3,2,1,0:T(8,128)(2,1)} %bitcast.13), channel_id=1, replica_groups=mesh['y'=4,'z'=8,'x'=4,'c'=2] {'c'}, dimensions={0} | all-to-all | bytes 524288 | tf_op jit(solution)/shard_map/all_to_all | solution.py:326
  206.3 1.9 final.1
  (92 shorter events, 12.6 us)
Async XLA Ops:
  0.0 66.4 %copy-start = (bf16[64,1024]{1,0:T(8,128)(2,1)S(1)}, bf16[64,1024]{1,0:T(8,128)(2,1)}, u32[]{:S(2)}) copy-start(bf16[64,1024]{1,0:T(8,128)(2,1)} %param.20) | copy-start | bytes 393220
  0.0 16.0 %copy-start.3 = (bf16[256,2048]{1,0:T(8,128)(2,1)S(1)}, bf16[256,2048]{1,0:T(8,128)(2,1)}, u32[]{:S(2)}) copy-start(bf16[256,2048]{1,0:T(8,128)(2,1)} %refs_7_.1) | copy-start | bytes 3145732
  0.0 55.5 %copy-start.17 = (s32[8]{0:T(128)S(1)}, s32[8]{0:T(128)}, u32[]{:S(2)}) copy-start(s32[8]{0:T(128)} %param.18) | copy-start | bytes 100
  2.8 4.7 %collective-permute-start = (bf16[4,3,128,128]{3,2,1,0:T(8,128)(2,1)}, bf16[4,3,128,128]{3,2,1,0:T(8,128)(2,1)S(1)}, u32[]{:S(2)}, u32[]{:S(2)}) collective-permute-start(bf16[4,3,128,128]{3,2,1,0:T(8,128)(2,1)} %get-tuple-element.24), channel_id=1, source_target_pairs={{0,1},{1,0},{2,3},{3,2},{4,5},{5,4},{6,7},{7,6},{8,9},{9,8},{10,11... | collective-permute-start | bytes 1179656 | tf_op jit(solution)/shard_map/ppermute | solution.py:330
  6.0 48.7 %collective-permute-start.12 = (bf16[256,2048]{1,0:T(8,128)(2,1)}, bf16[256,2048]{1,0:T(8,128)(2,1)}, u32[]{:S(2)}, u32[]{:S(2)}) collective-permute-start(bf16[256,2048]{1,0:T(8,128)(2,1)} %refs_7_.1), channel_id=1, source_target_pairs={{0,2},{2,4},{4,6},{6,0},{1,3},{3,5},{5,7},{7,1},{8,10},{10,12},{12... | collective-permute-start | bytes 3145736 | tf_op jit(solution)/shard_map/ppermute | solution.py:335
  9.5 65.8 %all-to-all-start = ((bf16[8,3,128,128]{3,2,1,0:T(8,128)(2,1)}), bf16[8,3,128,128]{3,2,1,0:T(8,128)(2,1)S(1)}, u32[]{:S(2)}, u32[]{:S(2)}) async-start(bf16[8,3,128,128]{3,2,1,0:T(8,128)(2,1)} %pad_maximum_fusion), calls=%async_computation | async-start | bytes 1572864 | tf_op jit(solution)/shard_map/all_to_all | solution.py:326
  16.0 69.7 %collective-permute-start.13 = (bf16[256,2048]{1,0:T(8,128)(2,1)S(1)}, bf16[256,2048]{1,0:T(8,128)(2,1)}, u32[]{:S(2)}, u32[]{:S(2)}) collective-permute-start(bf16[256,2048]{1,0:T(8,128)(2,1)S(1)} %copy-done.3), channel_id=1, source_target_pairs={{0,4},{2,6},{4,0},{6,2},{1,5},{3,7},{5,1},{7,3},{8,12},{10,14},{12... | collective-permute-start | bytes 3145736 | tf_op jit(solution)/shard_map/ppermute | solution.py:335
  18.9 67.3 %collective-permute-start.14 = (bf16[256,2048]{1,0:T(8,128)(2,1)S(1)}, bf16[256,2048]{1,0:T(8,128)(2,1)}, u32[]{:S(2)}, u32[]{:S(2)}) collective-permute-start(bf16[256,2048]{1,0:T(8,128)(2,1)S(1)} %copy-done.3), channel_id=1, source_target_pairs={{0,6},{2,0},{4,2},{6,4},{1,7},{3,1},{5,3},{7,5},{8,14},{10,8},{12,... | collective-permute-start | bytes 3145736 | tf_op jit(solution)/shard_map/ppermute | solution.py:335
  19.7 66.8 %collective-permute-start.15 = (bf16[256,2048]{1,0:T(8,128)(2,1)S(1)}, bf16[256,2048]{1,0:T(8,128)(2,1)}, u32[]{:S(2)}, u32[]{:S(2)}) collective-permute-start(bf16[256,2048]{1,0:T(8,128)(2,1)S(1)} %copy-done.3), channel_id=1, source_target_pairs={{0,1},{1,0},{2,3},{3,2},{4,5},{5,4},{6,7},{7,6},{8,9},{9,8},{10,11... | collective-permute-start | bytes 3145736 | tf_op jit(solution)/shard_map/ppermute | solution.py:330
  54.7 37.2 %collective-permute-start.16 = (bf16[256,2048]{1,0:T(8,128)(2,1)}, bf16[256,2048]{1,0:T(8,128)(2,1)}, u32[]{:S(2)}, u32[]{:S(2)}) collective-permute-start(bf16[256,2048]{1,0:T(8,128)(2,1)} %collective-permute-done.12.refs_8_), channel_id=1, source_target_pairs={{0,1},{1,0},{2,3},{3,2},{4,5},{5,4},{6,7},{7,6},{8,9},{9,8},{10,11... | collective-permute-start | bytes 3145736 | tf_op jit(solution)/shard_map/ppermute | solution.py:330
  55.5 2.6 %collective-permute-start.1 = (s32[8]{0:T(128)S(1)}, s32[8]{0:T(128)S(1)}, u32[]{:S(2)}, u32[]{:S(2)}) collective-permute-start(s32[8]{0:T(128)S(1)} %copy-done.17), channel_id=1, source_target_pairs={{0,1},{1,0},{2,3},{3,2},{4,5},{5,4},{6,7},{7,6},{8,9},{9,8},{10,11... | collective-permute-start | bytes 104 | tf_op jit(solution)/shard_map/ppermute | solution.py:330
  58.2 3.6 %collective-permute-start.2 = (s32[2,8]{1,0:T(2,128)S(1)}, s32[2,8]{1,0:T(2,128)S(1)}, u32[]{:S(2)}, u32[]{:S(2)}) collective-permute-start(s32[2,8]{1,0:T(2,128)S(1)} %get-tuple-element.46), channel_id=1, source_target_pairs={{0,2},{2,4},{4,6},{6,0},{1,3},{3,5},{5,7},{7,1},{8,10},{10,12},{12... | collective-permute-start | bytes 200 | tf_op jit(solution)/shard_map/ppermute | solution.py:335
  61.8 3.9 %collective-permute-start.3 = (s32[2,8]{1,0:T(2,128)S(1)}, s32[2,8]{1,0:T(2,128)S(1)}, u32[]{:S(2)}, u32[]{:S(2)}) collective-permute-start(s32[2,8]{1,0:T(2,128)S(1)} %get-tuple-element.46), channel_id=1, source_target_pairs={{0,4},{2,6},{4,0},{6,2},{1,5},{3,7},{5,1},{7,3},{8,12},{10,14},{12... | collective-permute-start | bytes 200 | tf_op jit(solution)/shard_map/ppermute | solution.py:335
  65.7 2.4 %collective-permute-start.4 = (s32[2,8]{1,0:T(2,128)S(1)}, s32[2,8]{1,0:T(2,128)S(1)}, u32[]{:S(2)}, u32[]{:S(2)}) collective-permute-start(s32[2,8]{1,0:T(2,128)S(1)} %get-tuple-element.46), channel_id=1, source_target_pairs={{0,6},{2,0},{4,2},{6,4},{1,7},{3,1},{5,3},{7,5},{8,14},{10,8},{12,... | collective-permute-start | bytes 200 | tf_op jit(solution)/shard_map/ppermute | solution.py:335
  71.6 25.8 %copy-start.12 = (s32[3]{0:T(128)S(1)}, s32[3]{0:T(128)}, u32[]{:S(2)}) copy-start(s32[3]{0:T(128)} %pad_add_fusion.2.where) | copy-start | bytes 40
  75.3 49.6 %copy-start.5 = (bf16[256,512]{1,0:T(8,128)(2,1)S(1)}, bf16[256,512]{1,0:T(8,128)(2,1)}, u32[]{:S(2)}) copy-start(bf16[256,512]{1,0:T(8,128)(2,1)} %refs_12_.1) | copy-start | bytes 786436
  76.2 17.8 %collective-permute-start.5 = (bf16[8,2,128,128]{3,2,1,0:T(8,128)(2,1)S(1)}, bf16[8,2,128,128]{3,2,1,0:T(8,128)(2,1)S(1)}, u32[]{:S(2)}, u32[]{:S(2)}) collective-permute-start(bf16[8,2,128,128]{3,2,1,0:T(8,128)(2,1)S(1)} %slice.22.kv), channel_id=1, source_target_pairs={{0,1},{1,0},{2,3},{3,2},{4,5},{5,4},{6,7},{7,6},{8,9},{9,8},{10,11... | collective-permute-start | bytes 1572872 | tf_op jit(solution)/shard_map/ppermute | solution.py:330
  80.2 36.5 %all-to-all-start.1 = ((bf16[8,40,1024]{2,1,0:T(8,128)(2,1)}), bf16[8,40,1024]{2,1,0:T(8,128)(2,1)}, u32[]{:S(2)}, u32[]{:S(2)}) async-start(bf16[8,40,1024]{2,1,0:T(8,128)(2,1)} %prep.1), calls=%async_computation.1 | async-start | bytes 1310720 | tf_op jit(solution)/shard_map/all_to_all | solution.py:326
  85.8 32.0 %collective-permute-start.17 = (bf16[256,2048]{1,0:T(8,128)(2,1)}, bf16[256,2048]{1,0:T(8,128)(2,1)}, u32[]{:S(2)}, u32[]{:S(2)}) collective-permute-start(bf16[256,2048]{1,0:T(8,128)(2,1)} %collective-permute-done.13.refs_9_), channel_id=1, source_target_pairs={{0,1},{1,0},{2,3},{3,2},{4,5},{5,4},{6,7},{7,6},{8,9},{9,8},{10,11... | collective-permute-start | bytes 3145736 | tf_op jit(solution)/shard_map/ppermute | solution.py:330
  86.2 32.6 %collective-permute-start.18 = (bf16[256,2048]{1,0:T(8,128)(2,1)}, bf16[256,2048]{1,0:T(8,128)(2,1)}, u32[]{:S(2)}, u32[]{:S(2)}) collective-permute-start(bf16[256,2048]{1,0:T(8,128)(2,1)} %collective-permute-done.14.refs_10_), channel_id=1, source_target_pairs={{0,1},{1,0},{2,3},{3,2},{4,5},{5,4},{6,7},{7,6},{8,9},{9,8},{10,11... | collective-permute-start | bytes 3145736 | tf_op jit(solution)/shard_map/ppermute | solution.py:330
  86.5 26.8 %collective-permute-start.10 = (bf16[8,2,128,128]{3,2,1,0:T(8,128)(2,1)S(1)}, bf16[8,2,128,128]{3,2,1,0:T(8,128)(2,1)}, u32[]{:S(2)}, u32[]{:S(2)}) collective-permute-start(bf16[8,2,128,128]{3,2,1,0:T(8,128)(2,1)S(1)} %slice.22.kv), channel_id=1, source_target_pairs={{0,192},{1,193},{2,194},{3,195},{4,196},{5,197},{6,198},{7,199},{8... | collective-permute-start | bytes 1572872 | tf_op jit(solution)/shard_map/ppermute | solution.py:340
  91.9 22.6 %collective-permute-start.6 = (bf16[8,2,128,128]{3,2,1,0:T(8,128)(2,1)S(1)}, bf16[8,2,128,128]{3,2,1,0:T(8,128)(2,1)}, u32[]{:S(2)}, u32[]{:S(2)}) collective-permute-start(bf16[8,2,128,128]{3,2,1,0:T(8,128)(2,1)S(1)} %slice.22.kv), channel_id=1, source_target_pairs={{0,64},{64,128},{128,192},{1,65},{65,129},{129,193},{2,66},{66,130... | collective-permute-start | bytes 1572872 | tf_op jit(solution)/shard_map/ppermute | solution.py:340
  94.0 21.4 %collective-permute-start.8 = (bf16[8,2,128,128]{3,2,1,0:T(8,128)(2,1)S(1)}, bf16[8,2,128,128]{3,2,1,0:T(8,128)(2,1)}, u32[]{:S(2)}, u32[]{:S(2)}) collective-permute-start(bf16[8,2,128,128]{3,2,1,0:T(8,128)(2,1)S(1)} %slice.22.kv), channel_id=1, source_target_pairs={{0,128},{64,192},{1,129},{65,193},{2,130},{66,194},{3,131},{67,195... | collective-permute-start | bytes 1572872 | tf_op jit(solution)/shard_map/ppermute | solution.py:340
  113.3 9.0 %collective-permute-start.11 = (bf16[8,2,128,128]{3,2,1,0:T(8,128)(2,1)}, bf16[8,2,128,128]{3,2,1,0:T(8,128)(2,1)}, u32[]{:S(2)}, u32[]{:S(2)}) collective-permute-start(bf16[8,2,128,128]{3,2,1,0:T(8,128)(2,1)} %collective-permute-done.10.refs_4_), channel_id=1, source_target_pairs={{0,1},{1,0},{2,3},{3,2},{4,5},{5,4},{6,7},{7,6},{8,9},{9,8},{10,11... | collective-permute-start | bytes 1572872 | tf_op jit(solution)/shard_map/ppermute | solution.py:330
  114.5 8.3 %collective-permute-start.7 = (bf16[8,2,128,128]{3,2,1,0:T(8,128)(2,1)}, bf16[8,2,128,128]{3,2,1,0:T(8,128)(2,1)}, u32[]{:S(2)}, u32[]{:S(2)}) collective-permute-start(bf16[8,2,128,128]{3,2,1,0:T(8,128)(2,1)} %collective-permute-done.6.refs_0_), channel_id=1, source_target_pairs={{0,1},{1,0},{2,3},{3,2},{4,5},{5,4},{6,7},{7,6},{8,9},{9,8},{10,11... | collective-permute-start | bytes 1572872 | tf_op jit(solution)/shard_map/ppermute | solution.py:330
  115.4 9.5 %collective-permute-start.9 = (bf16[8,2,128,128]{3,2,1,0:T(8,128)(2,1)}, bf16[8,2,128,128]{3,2,1,0:T(8,128)(2,1)}, u32[]{:S(2)}, u32[]{:S(2)}) collective-permute-start(bf16[8,2,128,128]{3,2,1,0:T(8,128)(2,1)} %collective-permute-done.8.refs_2_), channel_id=1, source_target_pairs={{0,1},{1,0},{2,3},{3,2},{4,5},{5,4},{6,7},{7,6},{8,9},{9,8},{10,11... | collective-permute-start | bytes 1572872 | tf_op jit(solution)/shard_map/ppermute | solution.py:330
  117.8 52.9 %collective-permute-start.30 = (bf16[8,32,1024]{2,1,0:T(8,128)(2,1)S(1)}, bf16[8,32,1024]{2,1,0:T(8,128)(2,1)S(1)}, u32[]{:S(2)}, u32[]{:S(2)}) collective-permute-start(bf16[8,32,1024]{2,1,0:T(8,128)(2,1)S(1)} %slice.27.refs_8_), channel_id=1, source_target_pairs={{0,64},{64,128},{128,192},{192,0},{1,65},{65,129},{129,193},{193,1... | collective-permute-start | bytes 1572872 | tf_op jit(solution)/shard_map/ppermute | solution.py:335
  118.8 16.6 %collective-permute-start.20 = (bf16[8,8,1024]{2,1,0:T(8,128)(2,1)S(1)}, bf16[8,8,1024]{2,1,0:T(8,128)(2,1)S(1)}, u32[]{:S(2)}, u32[]{:S(2)}) collective-permute-start(bf16[8,8,1024]{2,1,0:T(8,128)(2,1)S(1)} %slice.26.e0), channel_id=1, source_target_pairs={{0,64},{64,128},{128,192},{192,0},{1,65},{65,129},{129,193},{193,1... | collective-permute-start | bytes 393224 | tf_op jit(solution)/shard_map/ppermute | solution.py:335
  122.4 17.2 %collective-permute-start.21 = (bf16[8,8,1024]{2,1,0:T(8,128)(2,1)S(1)}, bf16[8,8,1024]{2,1,0:T(8,128)(2,1)S(1)}, u32[]{:S(2)}, u32[]{:S(2)}) collective-permute-start(bf16[8,8,1024]{2,1,0:T(8,128)(2,1)S(1)} %slice.26.e0), channel_id=1, source_target_pairs={{0,128},{64,192},{128,0},{192,64},{1,129},{65,193},{129,1},{193,65... | collective-permute-start | bytes 393224 | tf_op jit(solution)/shard_map/ppermute | solution.py:335
  122.8 16.8 %collective-permute-start.22 = (bf16[8,8,1024]{2,1,0:T(8,128)(2,1)S(1)}, bf16[8,8,1024]{2,1,0:T(8,128)(2,1)S(1)}, u32[]{:S(2)}, u32[]{:S(2)}) collective-permute-start(bf16[8,8,1024]{2,1,0:T(8,128)(2,1)S(1)} %slice.26.e0), channel_id=1, source_target_pairs={{0,192},{64,0},{128,64},{192,128},{1,193},{65,1},{129,65},{193,129... | collective-permute-start | bytes 393224 | tf_op jit(solution)/shard_map/ppermute | solution.py:335
  124.9 14.7 %copy-start.13 = (f32[2048]{0:T(1024)S(1)}, f32[2048]{0:T(1024)}, u32[]{:S(2)}) copy-start(f32[2048]{0:T(1024)} %param.22) | copy-start | bytes 24580
  124.9 14.7 %copy-start.14 = (s32[4]{0:T(128)S(1)}, s32[4]{0:T(128)}, u32[]{:S(2)}) copy-start(s32[4]{0:T(128)} %off.5) | copy-start | bytes 52
  124.9 21.7 %collective-permute-start.19 = (bf16[64,512]{1,0:T(8,128)(2,1)S(1)}, bf16[64,512]{1,0:T(8,128)(2,1)S(1)}, u32[]{:S(2)}, u32[]{:S(2)}) collective-permute-start(bf16[64,512]{1,0:T(8,128)(2,1)S(1)} %slice.25), channel_id=1, source_target_pairs={{8,0},{16,8},{24,16},{32,24},{40,32},{48,40},{56,48},{64,56},{72,6... | collective-permute-start | bytes 196616 | tf_op jit(solution)/shard_map/ppermute | solution.py:362
  131.9 20.3 %copy-start.10 = (bf16[8,128,128]{2,1,0:T(8,128)(2,1)}, bf16[8,128,128]{2,1,0:T(8,128)(2,1)S(1)}, u32[]{:S(2)}) copy-start(bf16[8,128,128]{2,1,0:T(8,128)(2,1)S(1)} %get-tuple-element.32) | copy-start | bytes 786436
  146.6 12.3 %collective-permute-start.23 = (bf16[1024,128]{1,0:T(8,128)(2,1)S(1)}, bf16[1024,128]{1,0:T(8,128)(2,1)S(1)}, u32[]{:S(2)}, u32[]{:S(2)}) collective-permute-start(bf16[1024,128]{1,0:T(8,128)(2,1)S(1)} %encode.1.refs_0_), channel_id=1, source_target_pairs={{0,2},{2,4},{4,6},{6,0},{1,3},{3,5},{5,7},{7,1},{8,10},{10,12},{12... | collective-permute-start | bytes 786440 | tf_op jit(solution)/shard_map/ppermute | solution.py:335
  147.4 15.1 %collective-permute-start.24 = (bf16[1024,128]{1,0:T(8,128)(2,1)S(1)}, bf16[1024,128]{1,0:T(8,128)(2,1)S(1)}, u32[]{:S(2)}, u32[]{:S(2)}) collective-permute-start(bf16[1024,128]{1,0:T(8,128)(2,1)S(1)} %encode.1.refs_0_), channel_id=1, source_target_pairs={{0,4},{2,6},{4,0},{6,2},{1,5},{3,7},{5,1},{7,3},{8,12},{10,14},{12... | collective-permute-start | bytes 786440 | tf_op jit(solution)/shard_map/ppermute | solution.py:335
  151.0 17.4 %collective-permute-start.25 = (bf16[1024,128]{1,0:T(8,128)(2,1)S(1)}, bf16[1024,128]{1,0:T(8,128)(2,1)}, u32[]{:S(2)}, u32[]{:S(2)}) collective-permute-start(bf16[1024,128]{1,0:T(8,128)(2,1)S(1)} %encode.1.refs_0_), channel_id=1, source_target_pairs={{0,6},{2,0},{4,2},{6,4},{1,7},{3,1},{5,3},{7,5},{8,14},{10,8},{12,... | collective-permute-start | bytes 786440 | tf_op jit(solution)/shard_map/ppermute | solution.py:335
  151.0 19.5 %collective-permute-start.26 = (bf16[1024,128]{1,0:T(8,128)(2,1)S(1)}, bf16[1024,128]{1,0:T(8,128)(2,1)}, u32[]{:S(2)}, u32[]{:S(2)}) collective-permute-start(bf16[1024,128]{1,0:T(8,128)(2,1)S(1)} %encode.1.refs_0_), channel_id=1, source_target_pairs={{0,1},{1,0},{2,3},{3,2},{4,5},{5,4},{6,7},{7,6},{8,9},{9,8},{10,11... | collective-permute-start | bytes 786440 | tf_op jit(solution)/shard_map/ppermute | solution.py:330
  152.2 46.4 %all-to-all-start.2 = ((bf16[8,128,128]{2,1,0:T(8,128)(2,1)}), bf16[8,128,128]{2,1,0:T(8,128)(2,1)}, u32[]{:S(2)}, u32[]{:S(2)}) async-start(bf16[8,128,128]{2,1,0:T(8,128)(2,1)} %copy-done.10), calls=%async_computation.2 | async-start | bytes 524288 | tf_op jit(solution)/shard_map/all_to_all | solution.py:326
  158.9 19.7 %copy-start.6 = (bf16[1024,128]{1,0:T(8,128)(2,1)}, bf16[1024,128]{1,0:T(8,128)(2,1)S(1)}, u32[]{:S(2)}) copy-start(bf16[1024,128]{1,0:T(8,128)(2,1)S(1)} %collective-permute-done.23.refs_1_) | copy-start | bytes 786436
  158.9 19.7 %collective-permute-start.31 = (bf16[8,32,1024]{2,1,0:T(8,128)(2,1)S(1)}, bf16[8,32,1024]{2,1,0:T(8,128)(2,1)S(1)}, u32[]{:S(2)}, u32[]{:S(2)}) collective-permute-start(bf16[8,32,1024]{2,1,0:T(8,128)(2,1)S(1)} %slice.27.refs_8_), channel_id=1, source_target_pairs={{0,128},{64,192},{128,0},{192,64},{1,129},{65,193},{129,1},{193,65... | collective-permute-start | bytes 1572872 | tf_op jit(solution)/shard_map/ppermute | solution.py:335
  162.4 16.1 %copy-start.8 = (bf16[1024,128]{1,0:T(8,128)(2,1)}, bf16[1024,128]{1,0:T(8,128)(2,1)S(1)}, u32[]{:S(2)}) copy-start(bf16[1024,128]{1,0:T(8,128)(2,1)S(1)} %collective-permute-done.24.refs_2_) | copy-start | bytes 786436
  162.5 25.5 %collective-permute-start.32 = (bf16[8,32,1024]{2,1,0:T(8,128)(2,1)S(1)}, bf16[8,32,1024]{2,1,0:T(8,128)(2,1)S(1)}, u32[]{:S(2)}, u32[]{:S(2)}) collective-permute-start(bf16[8,32,1024]{2,1,0:T(8,128)(2,1)S(1)} %slice.27.refs_8_), channel_id=1, source_target_pairs={{0,192},{64,0},{128,64},{192,128},{1,193},{65,1},{129,65},{193,129... | collective-permute-start | bytes 1572872 | tf_op jit(solution)/shard_map/ppermute | solution.py:335
  168.4 19.6 %collective-permute-start.27 = (bf16[1024,128]{1,0:T(8,128)(2,1)S(1)}, bf16[1024,128]{1,0:T(8,128)(2,1)S(1)}, u32[]{:S(2)}, u32[]{:S(2)}) collective-permute-start(bf16[1024,128]{1,0:T(8,128)(2,1)S(1)} %collective-permute-done.23.refs_1_), channel_id=1, source_target_pairs={{0,1},{1,0},{2,3},{3,2},{4,5},{5,4},{6,7},{7,6},{8,9},{9,8},{10,11... | collective-permute-start | bytes 786440 | tf_op jit(solution)/shard_map/ppermute | solution.py:330
  170.6 17.4 %collective-permute-start.28 = (bf16[1024,128]{1,0:T(8,128)(2,1)S(1)}, bf16[1024,128]{1,0:T(8,128)(2,1)S(1)}, u32[]{:S(2)}, u32[]{:S(2)}) collective-permute-start(bf16[1024,128]{1,0:T(8,128)(2,1)S(1)} %collective-permute-done.24.refs_2_), channel_id=1, source_target_pairs={{0,1},{1,0},{2,3},{3,2},{4,5},{5,4},{6,7},{7,6},{8,9},{9,8},{10,11... | collective-permute-start | bytes 786440 | tf_op jit(solution)/shard_map/ppermute | solution.py:330
  170.7 17.3 %collective-permute-start.29 = (bf16[1024,128]{1,0:T(8,128)(2,1)}, bf16[1024,128]{1,0:T(8,128)(2,1)S(1)}, u32[]{:S(2)}, u32[]{:S(2)}) collective-permute-start(bf16[1024,128]{1,0:T(8,128)(2,1)} %collective-permute-done.25.refs_3_), channel_id=1, source_target_pairs={{0,1},{1,0},{2,3},{3,2},{4,5},{5,4},{6,7},{7,6},{8,9},{9,8},{10,11... | collective-permute-start | bytes 786440 | tf_op jit(solution)/shard_map/ppermute | solution.py:330
  195.4 10.3 %copy-start.4 = (f32[256,512]{1,0:T(8,128)}, f32[256,512]{1,0:T(8,128)S(1)}, u32[]{:S(2)}) copy-start(f32[256,512]{1,0:T(8,128)S(1)} %get-tuple-element.39.cca) | copy-start | bytes 1572868
  195.4 10.2 %collective-permute-start.33 = (f32[64,512]{1,0:T(8,128)S(1)}, f32[64,512]{1,0:T(8,128)S(1)}, u32[]{:S(2)}, u32[]{:S(2)}) collective-permute-start(f32[64,512]{1,0:T(8,128)S(1)} %get-tuple-element.40), channel_id=1, source_target_pairs={{0,8},{8,16},{16,24},{24,32},{32,40},{40,48},{48,56},{56,64},{64,7... | collective-permute-start | bytes 393224 | tf_op jit(solution)/shard_map/ppermute | solution.py:402
  (7 other events, 10.9 us)
